TPU v7x, 256 devices: a whole 4x4x8 slice. The times are simulated.
256 devices in a mesh: ctx: 16 (over x_hi, y, core), head: 16 (over z, x_lo).
Axes of the slice: x: 4 (x_hi: 2, x_lo: 2; x = x_hi * 2 + x_lo), y: 4, z: 8, core: 2. Of those that a mesh axis runs over, the one named last changes fastest.
Arguments:
- queries: bfloat16 [32768, 2048], P(('ctx', 'head')), may hold values from -16 to 16
- keys: bfloat16 [32768, 512], P(('ctx', 'head')), may hold values from -4 to 4
- values: bfloat16 [32768, 512], P(('ctx', 'head')), may hold values from -6 to 6
- d_out: bfloat16 [32768, 2048], P(('ctx', 'head')), may hold values from -6 to 6
- lengths: int32 [32], replicated, may hold values from 1 to 8192, 32768 in all
Outputs:
- attn_out: bfloat16 [32768, 2048], P(('ctx', 'head'))
- grad_queries: bfloat16 [32768, 2048], P(('ctx', 'head'))
- grad_keys: bfloat16 [32768, 512], P(('ctx', 'head'))
- grad_values: bfloat16 [32768, 512], P(('ctx', 'head'))
Inputs may be any that keep to these rules, and one draw needn't show every extreme that they name: The 32 lengths sum to 32768; the longest is exactly 8192.
All inputs are finite; a program needn't handle non-finite values.
Results may differ from a plain program's by a relative error of at most 0.035.
Values may be sent and summed in bfloat16 or wider, within the bound.
A program may use at most 128 MiB of HBM per device.

v0:
```python
import functools
import math

import jax
import jax.numpy as jnp
from jax import lax
from jax.experimental import pallas as pl
from jax.experimental.pallas import tpu as pltpu
from jax.sharding import PartitionSpec as P

QH = 16
KVH = 4
HD = 128
GROUP = QH // KVH
SEQ = 32768
DOC_MOST = 8192
NEG_FILL = -1e30

XHI, YN, ZN, XLO = 2, 4, 8, 2
RING = 32
HALF = 64
PIECES = XHI * YN
ROWS = GROUP * HALF
KB = 512
KBLOCKS = SEQ // KB
SPAN = DOC_MOST // KB + 2

MESH = pl.DeviceIdType.MESH
ANY = pl.BlockSpec(memory_space=pl.ANY)
VMEM = pl.BlockSpec(memory_space=pltpu.VMEM)
SMEM = pl.BlockSpec(memory_space=pltpu.SMEM)


def here():
    c = lax.axis_index("ctx")
    h = lax.axis_index("head")
    xh, y, core = c // 8, lax.rem(c // 2, 4), lax.rem(c, 2)
    z, xl = h // 2, lax.rem(h, 2)
    return xh * 2 + xl, y, z, core


def device(x, y, z, core):
    return ((x // 2) * 8 + y * 2 + core, z * 2 + lax.rem(x, 2))


def ring_place(ring, n):
    major, minor = n // 4, lax.rem(n, 4)
    if ring == 0:
        return lax.rem(minor + 3 * major, 4), major
    return lax.rem(major, 4), lax.rem(3 * major + minor, 8)


def ring_number(ring, x, z):
    if ring == 0:
        return 4 * z + lax.rem(x + z, 4)
    part = lax.rem(z + 5 * x, 8)
    return 4 * x + part + 12 * (part // 4)


def greet(peers):
    barrier = pltpu.get_barrier_semaphore()
    for peer in peers:
        pl.semaphore_signal(barrier, inc=1, device_id=peer, device_id_type=MESH)
    pl.semaphore_wait(barrier, len(peers))


def remote(src, dst, send, recv, peer):
    return pltpu.make_async_remote_copy(
        src_ref=src, dst_ref=dst, send_sem=send, recv_sem=recv, device_id=peer, device_id_type=MESH
    )


def lanes(start, size):
    return pl.ds(pl.multiple_of(start * size, size), size)


class Spot:
    def __init__(self):
        self.x, self.y, self.z, self.core = here()
        self.xh, self.xl = self.x // 2, lax.rem(self.x, 2)
        self.number = [ring_number(r, self.x, self.z) for r in range(2)]
        self.next = []
        for flow in range(4):
            ring, step = flow // 2, 1 if flow % 2 == 0 else RING - 1
            x, z = ring_place(ring, lax.rem(self.number[ring] + step, RING))
            self.next.append(device(x, self.y, z, self.core))
        self.partner = device(self.x, self.y, self.z, 1 - self.core)
        self.offsets = [(dx, dy) for dx in range(XHI) for dy in range(YN)]

    def part_of(self, dx, dy):
        return lax.rem(self.xh + dx, XHI), lax.rem(self.y + dy, YN)

    def part_device(self, dx, dy):
        xh, y = self.part_of(dx, dy)
        return device(xh * 2 + self.xl, y, self.z, self.core)

    def peers(self):
        return (
            self.next + [self.partner] + [self.part_device(dx, dy) for dx, dy in self.offsets[1:]]
        )

    def chunk(self, ref, ring, n, core):
        x, z = ring_place(ring, n)
        return ref.at[x // 2, :, core * 16 + z * 2 + lax.rem(x, 2)]


def gather_kernel(
    q_ref, k_ref, v_ref, g_ref, ka_ref, va_ref, qi_ref, gi_ref,
    y_send, y_recv, p_send, p_recv, r_send, r_recv, c_send, c_recv, local,
):
    at = Spot()
    greet(at.peers())
    mine = at.core * 16 + at.z * 2 + at.xl
    ours = [ka_ref, va_ref]
    copies = []
    for number, (src, dst) in enumerate([(k_ref, ka_ref), (v_ref, va_ref)]):
        keep = pltpu.make_async_copy(
            src.at[:, lanes(at.y, HD)], dst.at[at.xh, at.y, mine], local.at[number]
        )
        keep.start()
        copies.append(keep)
        for dy in range(1, YN):
            _, y = at.part_of(0, dy)
            send = remote(
                src.at[:, lanes(y, HD)],
                dst.at[at.xh, at.y, mine],
                y_send.at[number, dy],
                y_recv.at[number, dy],
                at.part_device(0, dy),
            )
            send.start()
            copies.append(send)
    for copy in copies:
        copy.wait()

    def forward(flow, step):
        ring = flow // 2
        if flow % 2 == 0:
            origin = lax.rem(at.number[ring] - step + RING, RING)
        else:
            origin = lax.rem(at.number[ring] + step, RING)
        piece = at.chunk(ours[ring], ring, origin, at.core)
        return remote(
            piece, piece, r_send.at[flow, step], r_recv.at[flow, step + 1], at.next[flow]
        )

    def across(flow, step):
        ring = flow // 2
        if flow % 2 == 0:
            origin = lax.rem(at.number[ring] - step + RING, RING)
        else:
            origin = lax.rem(at.number[ring] + step, RING)
        piece = at.chunk(ours[ring], ring, origin, at.core)
        return remote(piece, piece, c_send.at[flow, step], c_recv.at[flow, step], at.partner)

    def arrived(flow, step):
        forward(flow, step - 1).wait_recv()

    for flow in range(4):
        forward(flow, 0).start()
    for flow in (0, 2):
        across(flow, 0).start()
    moves = []
    for number, (src, dst) in enumerate([(q_ref, qi_ref), (g_ref, gi_ref)]):
        for place, (dx, dy) in enumerate(at.offsets):
            xh, y = at.part_of(dx, dy)
            piece = src.at[pl.ds(pl.multiple_of(xh * HALF, HALF), HALF), lanes(y, GROUP * HD)]
            slot = dst.at[at.xh * YN + at.y]
            if place == 0:
                move = pltpu.make_async_copy(piece, slot, local.at[2 + number])
            else:
                move = remote(
                    piece,
                    slot,
                    p_send.at[number, place],
                    p_recv.at[number, place],
                    at.part_device(dx, dy),
                )
            move.start()
            moves.append(move)

    def step_body(step, carry):
        for flow in range(4):
            arrived(flow, step)
            forward(flow, step).start()
            across(flow, step).start()
        return carry

    lax.fori_loop(1, 15, step_body, 0)
    for flow in range(4):
        arrived(flow, 15)
        if flow % 2 == 0:
            forward(flow, 15).start()
        across(flow, 15).start()
    for flow in (0, 2):
        arrived(flow, 16)
        across(flow, 16).start()
    for move in moves:
        move.wait()

    def drain(step, carry):
        for flow in range(4):
            forward(flow, step).wait_send()
            across(flow, step).wait()
        return carry

    for flow in range(4):
        forward(flow, 0).wait_send()
    lax.fori_loop(1, 15, drain, 0)
    for flow in range(4):
        across(flow, 15).wait()
    for flow in (0, 2):
        forward(flow, 15).wait_send()
        across(flow, 0).wait()
        across(flow, 16).wait()


def gather(queries, keys, values, d_out):
    whole = jax.ShapeDtypeStruct((XHI, YN, 32, 128, HD), jnp.bfloat16)
    part = jax.ShapeDtypeStruct((PIECES, HALF, GROUP * HD), jnp.bfloat16)
    dma = pltpu.SemaphoreType.DMA
    return pl.pallas_call(
        gather_kernel,
        out_shape=(whole, whole, part, part),
        in_specs=[ANY] * 4,
        out_specs=(ANY,) * 4,
        scratch_shapes=[
            dma((2, YN)), dma((2, YN)), dma((2, PIECES)), dma((2, PIECES)),
            dma((4, 17)), dma((4, 17)), dma((4, 17)), dma((4, 17)), dma((4,)),
        ],
        compiler_params=pltpu.CompilerParams(collective_id=0, has_side_effects=True),
        name="gather",
    )(queries, keys, values, d_out)


def attention_kernel(
    meta, touched, start_ref, q_ref, g_ref, ka_ref, va_ref, o_ref, dq_ref, dk_ref, dv_ref,
    kbuf, vbuf, sbuf, pbuf, dk_acc, dv_acc, flush, k_sem, v_sem, f_sem,
):
    scaling = HD ** (-0.5)
    factor = scaling * math.log2(math.e)

    def rows_of(j):
        return pl.ds(pl.multiple_of(j * KB, KB), KB)

    def fetches(i, slot, j):
        src = rows_of(meta[i, 0] + j)
        return (
            pltpu.make_async_copy(ka_ref.at[src], kbuf.at[slot, rows_of(j)], k_sem.at[slot, j]),
            pltpu.make_async_copy(va_ref.at[src], vbuf.at[slot, rows_of(j)], v_sem.at[slot, j]),
        )

    def fetch(i, slot):
        def body(j, carry):
            for copy in fetches(i, slot, j):
                copy.start()
            return carry

        lax.fori_loop(0, meta[i, 1], body, 0)

    def stacked(value):
        return jnp.concatenate([value[:, h * HD : (h + 1) * HD] for h in range(GROUP)], axis=0)

    def unstacked(value):
        return jnp.concatenate([value[h * HALF : (h + 1) * HALF] for h in range(GROUP)], axis=1)

    def mm(a, b, da, db):
        return lax.dot_general(
            a, b, (((da,), (db,)), ((), ())), preferred_element_type=jnp.float32
        )

    fetch(0, 0)

    def piece(i, seen):
        slot = lax.rem(i, 2)

        @pl.when(i + 1 < PIECES)
        def _():
            fetch(i + 1, 1 - slot)

        low, count, first = meta[i, 0], meta[i, 1], meta[i, 2]
        q = stacked(q_ref[i])
        g = stacked(g_ref[i])
        starts = start_ref[i]
        times = first + lax.rem(lax.broadcasted_iota(jnp.int32, (1, ROWS), 1), HALF)
        key_iota = lax.broadcasted_iota(jnp.int32, (KB, ROWS), 0)

        def scores_step(j, top):
            fetches(i, slot, j)[0].wait()
            s = mm(kbuf[slot, rows_of(j)], q, 1, 1)
            base = (low + j) * KB
            s = jnp.where((key_iota >= starts - base) & (key_iota <= times - base), s, NEG_FILL)
            sbuf[rows_of(j)] = s
            return jnp.maximum(top, jnp.max(s.reshape(KB // 8, 8, ROWS), axis=0))

        top = lax.fori_loop(0, count, scores_step, jnp.full((8, ROWS), NEG_FILL, jnp.float32))
        top = jnp.max(top, axis=0, keepdims=True)

        def weights_step(j, carry):
            total, out = carry
            fetches(i, slot, j)[1].wait()
            p = jnp.exp2((sbuf[rows_of(j)] - top) * factor)
            total = total + jnp.sum(p.reshape(KB // 8, 8, ROWS), axis=0)
            p = p.astype(jnp.bfloat16)
            pbuf[rows_of(j)] = p
            return total, out + mm(vbuf[slot, rows_of(j)], p, 0, 0)

        total, out = lax.fori_loop(
            0,
            count,
            weights_step,
            (jnp.zeros((8, ROWS), jnp.float32), jnp.zeros((HD, ROWS), jnp.float32)),
        )
        inverse = 1.0 / jnp.sum(total, axis=0, keepdims=True)
        out = (out * inverse).astype(jnp.bfloat16).astype(jnp.float32)
        o_ref[i] = unstacked(out.T.astype(jnp.bfloat16))
        g_turned = g.astype(jnp.float32).T
        delta = jnp.sum(g_turned * out, axis=0, keepdims=True) * inverse
        g_turned = g_turned * inverse
        g_rows = g_turned.T.astype(jnp.bfloat16)

        def clear(kb, carry):
            dk_acc[rows_of(kb)] = jnp.zeros((KB, HD), jnp.float32)
            dv_acc[rows_of(kb)] = jnp.zeros((KB, HD), jnp.float32)
            return carry

        lax.fori_loop(jnp.maximum(low, seen), low + count, clear, 0)

        def grad_step(j, dq):
            k = kbuf[slot, rows_of(j)]
            p = pbuf[rows_of(j)]
            gp = mm(vbuf[slot, rows_of(j)], g_rows, 1, 1)
            ds = (p.astype(jnp.float32) * (gp - delta)).astype(jnp.bfloat16)
            where = rows_of(low + j)
            dv_acc[where] += mm(p, g_rows, 1, 0)
            dk_acc[where] += mm(ds, q, 1, 0)
            return dq + mm(k, ds, 0, 0)

        dq = lax.fori_loop(0, count, grad_step, jnp.zeros((HD, ROWS), jnp.float32))
        dq_ref[i] = unstacked((dq * scaling).T.astype(jnp.bfloat16))
        return low + count

    lax.fori_loop(0, PIECES, piece, 0)

    def flushes(kb, slot):
        return (
            pltpu.make_async_copy(flush.at[0, slot], dk_ref.at[rows_of(kb)], f_sem.at[0, slot]),
            pltpu.make_async_copy(flush.at[1, slot], dv_ref.at[rows_of(kb)], f_sem.at[1, slot]),
        )

    def flush_step(kb, carry):
        slot = lax.rem(kb, 2)

        @pl.when(kb >= 2)
        def _():
            for copy in flushes(kb - 2, slot):
                copy.wait()

        @pl.when(touched[kb] > 0)
        def _():
            flush[0, slot] = (dk_acc[rows_of(kb)] * scaling).astype(jnp.bfloat16)
            flush[1, slot] = dv_acc[rows_of(kb)].astype(jnp.bfloat16)

        @pl.when(touched[kb] == 0)
        def _():
            flush[0, slot] = jnp.zeros((KB, HD), jnp.bfloat16)
            flush[1, slot] = jnp.zeros((KB, HD), jnp.bfloat16)

        for copy in flushes(kb, slot):
            copy.start()
        return carry

    lax.fori_loop(0, KBLOCKS, flush_step, 0)
    for kb in (KBLOCKS - 2, KBLOCKS - 1):
        for copy in flushes(kb, kb % 2):
            copy.wait()


def attention(lengths, q, g, keys, values):
    x, y, z, core = here()
    ends = jnp.cumsum(lengths)
    part = jnp.arange(PIECES, dtype=jnp.int32)
    block = (part // YN) * 128 + lax.rem(part, YN) * 32 + core * 16 + z * 2 + lax.rem(x, 2)
    first = block * 128 + (x // 2) * HALF
    times = first[:, None] + jnp.arange(HALF, dtype=jnp.int32)[None, :]
    starts = jnp.sum(
        jnp.where(ends[None, None, :] <= times[:, :, None], lengths[None, None, :], 0), axis=2
    )
    low = starts[:, 0] // KB
    high = (first + HALF - 1) // KB
    meta = jnp.stack([low, high - low + 1, first], axis=1).astype(jnp.int32)
    block_ids = jnp.arange(KBLOCKS, dtype=jnp.int32)[:, None]
    touched = jnp.any((block_ids >= low[None]) & (block_ids <= high[None]), axis=1)
    start_rows = jnp.tile(starts, (1, GROUP)).reshape(PIECES, 1, ROWS).astype(jnp.int32)
    part_shape = jax.ShapeDtypeStruct((PIECES, HALF, GROUP * HD), jnp.bfloat16)
    whole = jax.ShapeDtypeStruct((SEQ, HD), jnp.bfloat16)
    dma = pltpu.SemaphoreType.DMA
    return pl.pallas_call(
        attention_kernel,
        out_shape=(part_shape, part_shape, whole, whole),
        in_specs=[SMEM, SMEM, VMEM, VMEM, VMEM, ANY, ANY],
        out_specs=(VMEM, VMEM, ANY, ANY),
        scratch_shapes=[
            pltpu.VMEM((2, SPAN * KB, HD), jnp.bfloat16),
            pltpu.VMEM((2, SPAN * KB, HD), jnp.bfloat16),
            pltpu.VMEM((SPAN * KB, ROWS), jnp.float32),
            pltpu.VMEM((SPAN * KB, ROWS), jnp.bfloat16),
            pltpu.VMEM((SEQ, HD), jnp.float32),
            pltpu.VMEM((SEQ, HD), jnp.float32),
            pltpu.VMEM((2, 2, KB, HD), jnp.bfloat16),
            dma((2, SPAN)),
            dma((2, SPAN)),
            dma((2, 2)),
        ],
        compiler_params=pltpu.CompilerParams(vmem_limit_bytes=62 << 20),
        name="attention",
    )(
        meta,
        touched.astype(jnp.int32),
        start_rows,
        q,
        g,
        keys.reshape(SEQ, HD),
        values.reshape(SEQ, HD),
    )


def scatter_kernel(
    o_ref, dq_ref, dk_ref, dv_ref, ao_ref, gq_ref, gk_ref, gv_ref,
    own, part, recv, done,
    own_sem, c_send, c_recv, r_send, r_recv, p_send, p_recv, y_send, y_recv, local,
):
    at = Spot()
    greet(at.peers())
    ours = [dk_ref, dv_ref]

    def target(flow, step):
        ring = flow // 2
        if flow % 2 == 0:
            return lax.rem(at.number[ring] + 17 - step, RING)
        return lax.rem(at.number[ring] + 16 + step, RING)

    def load(flow, step, n):
        piece = at.chunk(ours[flow // 2], flow // 2, n, at.core)
        return pltpu.make_async_copy(piece, own.at[flow, step], own_sem.at[flow, step])

    def across(flow, step, n):
        piece = at.chunk(ours[flow // 2], flow // 2, n, 1 - at.core)
        return remote(
            piece, part.at[flow, step], c_send.at[flow, step], c_recv.at[flow, step], at.partner
        )

    def forward(flow, step):
        return remote(
            own.at[flow, step],
            recv.at[flow, step - 1],
            r_send.at[flow, step - 1],
            r_recv.at[flow, step - 1],
            at.next[flow],
        )

    def begin(step, carry):
        for flow in range(4):
            load(flow, step, target(flow, step)).start()
            across(flow, step, target(flow, step)).start()
        return carry

    lax.fori_loop(1, 16, begin, 0)
    for flow in (0, 2):
        load(flow, 16, target(flow, 16)).start()
        across(flow, 16, target(flow, 16)).start()
        load(flow, 0, at.number[flow // 2]).start()
        across(flow, 0, at.number[flow // 2]).start()
    moves = []
    for number, (src, dst) in enumerate([(o_ref, ao_ref), (dq_ref, gq_ref)]):
        for place, (dx, dy) in enumerate(at.offsets):
            xh, y = at.part_of(dx, dy)
            piece = src.at[xh * YN + y]
            slot = dst.at[
                pl.ds(pl.multiple_of(at.xh * HALF, HALF), HALF), lanes(at.y, GROUP * HD)
            ]
            if place == 0:
                move = pltpu.make_async_copy(piece, slot, local.at[number])
            else:
                move = remote(
                    piece,
                    slot,
                    p_send.at[number, place],
                    p_recv.at[number, place],
                    at.part_device(dx, dy),
                )
            move.start()
            moves.append(move)

    def wide(ref, flow, step):
        return ref[flow, step].astype(jnp.float32)

    def ready(flow, step, n):
        load(flow, step, n).wait()
        across(flow, step, n).wait_recv()

    def send(flow, step, first):
        ready(flow, step, target(flow, step))
        total = wide(own, flow, step) + wide(part, flow, step)
        if not first:
            forward(flow, step - 1).wait_recv()
            total = total + wide(recv, flow, step - 2)
        own[flow, step] = total.astype(jnp.bfloat16)
        forward(flow, step).start()

    for flow in range(4):
        send(flow, 1, True)

    def step_body(step, carry):
        for flow in range(4):
            send(flow, step, False)
        return carry

    lax.fori_loop(2, 16, step_body, 0)
    for flow in (0, 2):
        send(flow, 16, False)
    for number, flow in enumerate((0, 2)):
        ready(flow, 0, at.number[number])
        total = wide(own, flow, 0) + wide(part, flow, 0)
        forward(flow, 16).wait_recv()
        forward(flow + 1, 15).wait_recv()
        total = total + wide(recv, flow, 15) + wide(recv, flow + 1, 14)
        done[number] = total.astype(jnp.bfloat16)
        dst = (gk_ref, gv_ref)[number]
        for dy in range(YN):
            _, y = at.part_of(0, dy)
            slot = dst.at[:, lanes(at.y, HD)]
            if dy == 0:
                move = pltpu.make_async_copy(done.at[number, y], slot, local.at[2 + number])
            else:
                move = remote(
                    done.at[number, y],
                    slot,
                    y_send.at[number, dy],
                    y_recv.at[number, dy],
                    at.part_device(0, dy),
                )
            move.start()
            moves.append(move)
    for move in moves:
        move.wait()

    def drain(step, carry):
        for flow in range(4):
            forward(flow, step).wait_send()
            across(flow, step, target(flow, step)).wait_send()
        return carry

    lax.fori_loop(1, 16, drain, 0)
    for flow in (0, 2):
        forward(flow, 16).wait_send()
        across(flow, 16, target(flow, 16)).wait_send()
        across(flow, 0, at.number[flow // 2]).wait_send()


def scatter(out, dq, dk, dv):
    tokens = jax.ShapeDtypeStruct((128, QH * HD), jnp.bfloat16)
    pairs = jax.ShapeDtypeStruct((128, KVH * HD), jnp.bfloat16)
    dma = pltpu.SemaphoreType.DMA
    slots = (YN, 128, HD)
    return pl.pallas_call(
        scatter_kernel,
        out_shape=(tokens, tokens, pairs, pairs),
        in_specs=[ANY] * 4,
        out_specs=(ANY,) * 4,
        scratch_shapes=[
            pltpu.VMEM((4, 17) + slots, jnp.bfloat16),
            pltpu.VMEM((4, 17) + slots, jnp.bfloat16),
            pltpu.VMEM((4, 16) + slots, jnp.bfloat16),
            pltpu.VMEM((2,) + slots, jnp.bfloat16),
            dma((4, 17)), dma((4, 17)), dma((4, 17)), dma((4, 16)), dma((4, 16)),
            dma((2, PIECES)), dma((2, PIECES)), dma((2, YN)), dma((2, YN)), dma((4,)),
        ],
        compiler_params=pltpu.CompilerParams(
            collective_id=1, has_side_effects=True, vmem_limit_bytes=48 << 20
        ),
        name="scatter",
    )(
        out,
        dq,
        dk.reshape(XHI, YN, 32, 128, HD),
        dv.reshape(XHI, YN, 32, 128, HD),
    )


def shards(queries, keys, values, d_out, lengths):
    ka, va, q, g = gather(queries, keys, values, d_out)
    out, dq, dk, dv = attention(lengths, q, g, ka, va)
    return scatter(out, dq, dk, dv)


def solution(mesh):
    spec = P(("ctx", "head"), None)
    return jax.shard_map(
        shards,
        mesh=mesh,
        in_specs=(spec, spec, spec, spec, P()),
        out_specs=(spec,) * 4,
        check_vma=False,
    )
```

profile of v0, /device:TPU:2, one launch (start us, length us, event | category | flops | bytes accessed | tf_op | source)
XLA Modules:
  0.0 297.7 jit_solution(8505491073424331591)
XLA Ops:
  0.7 0.1 iota_add_fusion
  0.8 0.7 copy.11
  1.5 0.1 reduce-window.8
  1.6 0.1 reduce
  1.7 0.8 select_reduce_fusion
  2.4 0.1 slice_reduce_fusion
  2.6 0.1 fusion.17
  2.7 0.5 convert_element_type.3.touched
  3.2 0.7 pad_add_fusion.meta
  3.9 0.7 tile.9.start_ref
  4.6 109.2 %gather.1 = (bf16[2,4,32,128,128]{4,3,2,1,0:T(8,128)(2,1)}, bf16[2,4,32,128,128]{4,3,2,1,0:T(8,128)(2,1)}, bf16[8,64,512]{2,1,0:T(8,128)(2,1)}, bf16[8,64,512]{2,1,0:T(8,128)(2,1)}) custom-call(bf16[128,2048]{1,0:T(8,128)(2,1)} %q_ref.1, bf16[128,512]{1,0:T(8,128)(2,1)} %k_ref.1, bf16[128,512]{1,0:T(8,128)(2,1)} %v_ref.1, bf16[128,2048]{1,0:T(8,128)(2,1)} %g_ref.1), custom_call_target="tpu_custom_call" | custom-call | tf_op jit(solution)/shard_map/gather/pallas_call | solution.py:222
  113.7 67.7 %attention.1 = (bf16[8,64,512]{2,1,0:T(8,128)(2,1)}, bf16[8,64,512]{2,1,0:T(8,128)(2,1)}, bf16[32768,128]{1,0:T(8,128)(2,1)}, bf16[32768,128]{1,0:T(8,128)(2,1)}) custom-call(s32[8,3]{1,0:T(8,128)} %pad_add_fusion.meta, s32[64]{0:T(128)} %convert_element_type.3.touched, s32[8,1,256]{2,1,0:T(1,128)} %tile.9.start_ref, ...), custom_call_target="tpu_custom_call" | custom-call | tf_op jit(solution)/shard_map/attention/pallas_call | solution.py:398
  181.5 0.0 copy-start
  181.5 1.0 copy-done
  182.5 0.0 copy-start.1
  182.5 1.0 copy-done.1
  183.6 111.2 %scatter.1 = (bf16[128,2048]{1,0:T(8,128)(2,1)S(1)}, bf16[128,2048]{1,0:T(8,128)(2,1)S(1)}, bf16[128,512]{1,0:T(8,128)(2,1)S(1)}, bf16[128,512]{1,0:T(8,128)(2,1)S(1)}) custom-call(bf16[8,64,512]{2,1,0:T(8,128)(2,1)S(1)} %copy-done, bf16[8,64,512]{2,1,0:T(8,128)(2,1)S(1)} %copy-done.1, bf16[2,4,32,128,128]{4,3,2,1,0:T(8,128)(2,1)} %bitcast.5, ...), custom_call_target="tpu_custom_call" | custom-call | tf_op jit(solution)/shard_map/scatter/pallas_call | solution.py:566
  294.8 0.8 copy.16
  295.6 0.8 copy.17
  296.4 0.7 copy.18
  297.0 0.7 copy.19
  (3 shorter events, 0.0 us)
Async XLA Ops:
  181.5 1.0 copy-start
  182.5 1.0 copy-start.1
where the time goes:
time: 299 us; the launch traced here: 298 us
  Pallas kernels  288 us (96%)
  local copies, waits for them, and re-layouts  6.4 us (2%)
    pallas_call x1, Pallas kernels, scatter(): pl.pallas_call(scatter_kernel, out_shape=(tokens, tokens, pairs, pairs),...  111 us
    pallas_call x1, Pallas kernels, gather(): pl.pallas_call(gather_kernel, out_shape=(whole, whole, part, part), in_sp...  109 us
    pallas_call x1, Pallas kernels, attention(): pl.pallas_call(attention_kernel, out_shape=(part_shape, part_shape, whole...  67.7 us

commit v1 on v0

--- a/solution.py
+++ b/solution.py
@@ -16,8 +16,8 @@
 DOC_MOST = 8192
 NEG_FILL = -1e30
 
-XHI, YN, ZN, XLO = 2, 4, 8, 2
-RING = 32
+XHI, XN, YN, ZN, XLO = 2, 4, 4, 8, 2
+WHOLE = (XHI, YN, 2, ZN, XLO, 128, 128)
 HALF = 64
 PIECES = XHI * YN
 ROWS = GROUP * HALF
@@ -43,20 +43,6 @@
     return ((x // 2) * 8 + y * 2 + core, z * 2 + lax.rem(x, 2))
 
 
-def ring_place(ring, n):
-    major, minor = n // 4, lax.rem(n, 4)
-    if ring == 0:
-        return lax.rem(minor + 3 * major, 4), major
-    return lax.rem(major, 4), lax.rem(3 * major + minor, 8)
-
-
-def ring_number(ring, x, z):
-    if ring == 0:
-        return 4 * z + lax.rem(x + z, 4)
-    part = lax.rem(z + 5 * x, 8)
-    return 4 * x + part + 12 * (part // 4)
-
-
 def greet(peers):
     barrier = pltpu.get_barrier_semaphore()
     for peer in peers:
@@ -78,14 +64,16 @@
     def __init__(self):
         self.x, self.y, self.z, self.core = here()
         self.xh, self.xl = self.x // 2, lax.rem(self.x, 2)
-        self.number = [ring_number(r, self.x, self.z) for r in range(2)]
-        self.next = []
-        for flow in range(4):
-            ring, step = flow // 2, 1 if flow % 2 == 0 else RING - 1
-            x, z = ring_place(ring, lax.rem(self.number[ring] + step, RING))
-            self.next.append(device(x, self.y, z, self.core))
+        self.x_peer = [device(self.x_at(d), self.y, self.z, self.core) for d in (1, -1)]
+        self.z_peer = [device(self.x, self.y, self.z_at(d), self.core) for d in (1, -1)]
         self.partner = device(self.x, self.y, self.z, 1 - self.core)
         self.offsets = [(dx, dy) for dx in range(XHI) for dy in range(YN)]
+
+    def x_at(self, d):
+        return lax.rem(self.x + d + XN, XN)
+
+    def z_at(self, d):
+        return lax.rem(self.z + d + ZN, ZN)
 
     def part_of(self, dx, dy):
         return lax.rem(self.xh + dx, XHI), lax.rem(self.y + dy, YN)
@@ -96,70 +84,117 @@
 
     def peers(self):
         return (
-            self.next + [self.partner] + [self.part_device(dx, dy) for dx, dy in self.offsets[1:]]
+            self.x_peer
+            + self.z_peer
+            + [self.partner]
+            + [self.part_device(dx, dy) for dx, dy in self.offsets[1:]]
         )
 
-    def chunk(self, ref, ring, n, core):
-        x, z = ring_place(ring, n)
-        return ref.at[x // 2, :, core * 16 + z * 2 + lax.rem(x, 2)]
+    def across_x(self, ref, core, dz, half=None):
+        return ref.at[:, halves(half), core, self.z_at(dz)]
+
+    def chunk(self, ref, dx, dz, half=None):
+        x = self.x_at(dx)
+        return ref.at[x // 2, halves(half), self.core, self.z_at(dz), lax.rem(x, 2)]
+
+
+def halves(half):
+    return pl.ds(0, YN) if half is None else pl.ds(half * 2, 2)
 
 
 def gather_kernel(
     q_ref, k_ref, v_ref, g_ref, ka_ref, va_ref, qi_ref, gi_ref,
-    y_send, y_recv, p_send, p_recv, r_send, r_recv, c_send, c_recv, local,
+    y_send, y_recv, p_send, p_recv, kx_send, kx_recv, kz_send, kz_recv, vz_send, vz_recv,
+    vx_send, vx_recv, c_send, c_recv, local,
 ):
     at = Spot()
     greet(at.peers())
-    mine = at.core * 16 + at.z * 2 + at.xl
-    ours = [ka_ref, va_ref]
     copies = []
-    for number, (src, dst) in enumerate([(k_ref, ka_ref), (v_ref, va_ref)]):
-        keep = pltpu.make_async_copy(
-            src.at[:, lanes(at.y, HD)], dst.at[at.xh, at.y, mine], local.at[number]
-        )
+    for number, (src, dst) in enumerate([(v_ref, va_ref), (k_ref, ka_ref)]):
+        slot = dst.at[at.xh, at.y, at.core, at.z, at.xl]
+        keep = pltpu.make_async_copy(src.at[:, lanes(at.y, HD)], slot, local.at[number])
         keep.start()
-        copies.append(keep)
+        copies.append([keep])
         for dy in range(1, YN):
             _, y = at.part_of(0, dy)
             send = remote(
                 src.at[:, lanes(y, HD)],
-                dst.at[at.xh, at.y, mine],
+                slot,
                 y_send.at[number, dy],
                 y_recv.at[number, dy],
                 at.part_device(0, dy),
             )
             send.start()
-            copies.append(send)
-    for copy in copies:
+            copies[number].append(send)
+
+    sent, crossing = [], []
+
+    def go(piece, send, recv, peer):
+        copy = remote(piece, piece, send, recv, peer)
+        copy.start()
+        sent.append(copy)
+        return copy
+
+    def cross(piece):
+        number = len(crossing)
+        crossing.append(go(piece, c_send.at[number], c_recv.at[number], at.partner))
+
+    def kx(number, piece, way):
+        return go(piece, kx_send.at[number], kx_recv.at[number], at.x_peer[way])
+
+    def kz(step, half, way):
+        dz = (1 - step) if way == 0 else (step - 1)
+        piece = at.across_x(ka_ref, at.core, dz, half)
+        place = (way, step, half)
+        return go(piece, kz_send.at[place], kz_recv.at[place], at.z_peer[way])
+
+    def vz(step, way):
+        dz = (1 - step) if way == 0 else (step - 1)
+        piece = at.chunk(va_ref, 0, dz, way if step == 4 else None)
+        return go(piece, vz_send.at[way, step], vz_recv.at[way, step], at.z_peer[way])
+
+    vx_first, vx_second = {}, {}
+
+    def vx(stage, way, dz, piece):
+        place = (stage, way, dz + 3)
+        return go(piece, vx_send.at[place], vx_recv.at[place], at.x_peer[way])
+
+    def vx_start(dz):
+        vx_first[dz] = [vx(0, way, dz, at.chunk(va_ref, 0, dz)) for way in range(2)]
+
+    def vx_forward(dz):
+        vx_second[dz] = []
+        for way in range(2):
+            vx_first[dz][way].wait_recv()
+            piece = at.chunk(va_ref, 2 * way - 1, dz, way)
+            vx_second[dz].append(vx(1, way, dz, piece))
+
+    def vx_end(dz):
+        for copy in vx_second[dz]:
+            copy.wait_recv()
+        cross(at.across_x(va_ref, at.core, dz))
+
+    def kz_step(before, step):
+        after = {}
+        for half in range(2):
+            for way in range(2):
+                if (half, way) not in before:
+                    continue
+                before[half, way].wait_recv()
+                if step < 4 or (step == 4 and half == way):
+                    after[half, way] = kz(step, half, way)
+                dz = (1 - step) if way == 0 else (step - 1)
+                cross(at.across_x(ka_ref, at.core, dz, half))
+        return after
+
+    for copy in copies[0]:
         copy.wait()
-
-    def forward(flow, step):
-        ring = flow // 2
-        if flow % 2 == 0:
-            origin = lax.rem(at.number[ring] - step + RING, RING)
-        else:
-            origin = lax.rem(at.number[ring] + step, RING)
-        piece = at.chunk(ours[ring], ring, origin, at.core)
-        return remote(
-            piece, piece, r_send.at[flow, step], r_recv.at[flow, step + 1], at.next[flow]
-        )
-
-    def across(flow, step):
-        ring = flow // 2
-        if flow % 2 == 0:
-            origin = lax.rem(at.number[ring] - step + RING, RING)
-        else:
-            origin = lax.rem(at.number[ring] + step, RING)
-        piece = at.chunk(ours[ring], ring, origin, at.core)
-        return remote(piece, piece, c_send.at[flow, step], c_recv.at[flow, step], at.partner)
-
-    def arrived(flow, step):
-        forward(flow, step - 1).wait_recv()
-
-    for flow in range(4):
-        forward(flow, 0).start()
-    for flow in (0, 2):
-        across(flow, 0).start()
+    v_step = [vz(1, way) for way in range(2)]
+    vx_start(0)
+    for copy in copies[1]:
+        copy.wait()
+    k_first = [kx(way, at.chunk(ka_ref, 0, 0), way) for way in range(2)]
+
     moves = []
     for number, (src, dst) in enumerate([(q_ref, qi_ref), (g_ref, gi_ref)]):
         for place, (dx, dy) in enumerate(at.offsets):
@@ -179,44 +214,57 @@
             move.start()
             moves.append(move)
 
-    def step_body(step, carry):
-        for flow in range(4):
-            arrived(flow, step)
-            forward(flow, step).start()
-            across(flow, step).start()
-        return carry
-
-    lax.fori_loop(1, 15, step_body, 0)
-    for flow in range(4):
-        arrived(flow, 15)
-        if flow % 2 == 0:
-            forward(flow, 15).start()
-        across(flow, 15).start()
-    for flow in (0, 2):
-        arrived(flow, 16)
-        across(flow, 16).start()
+    k_second = []
+    for way in range(2):
+        k_first[way].wait_recv()
+        k_second.append(kx(2 + way, at.chunk(ka_ref, 2 * way - 1, 0, way), way))
+
+    def vz_next(step):
+        for way in range(2):
+            v_step[way].wait_recv()
+            v_step[way] = vz(step, way)
+            vx_start((1 - step) if way == 0 else (step - 1))
+
+    vz_next(2)
+    for copy in k_second:
+        copy.wait_recv()
+    k_step = {(half, way): kz(1, half, way) for half in range(2) for way in range(2)}
+    cross(at.across_x(ka_ref, at.core, 0))
+    vz_next(3)
+    vx_forward(0)
+    vz_next(4)
+    vx_forward(-1)
+    vx_forward(1)
+    vx_end(0)
+    for way in range(2):
+        v_step[way].wait_recv()
+    vx_start(4)
+    k_step = kz_step(k_step, 2)
+    vx_forward(-2)
+    vx_forward(2)
+    vx_end(-1)
+    vx_end(1)
+    k_step = kz_step(k_step, 3)
+    vx_forward(-3)
+    vx_forward(3)
+    vx_end(-2)
+    vx_end(2)
+    k_step = kz_step(k_step, 4)
+    vx_forward(4)
+    vx_end(-3)
+    vx_end(3)
+    vx_end(4)
+    kz_step(k_step, 5)
     for move in moves:
         move.wait()
-
-    def drain(step, carry):
-        for flow in range(4):
-            forward(flow, step).wait_send()
-            across(flow, step).wait()
-        return carry
-
-    for flow in range(4):
-        forward(flow, 0).wait_send()
-    lax.fori_loop(1, 15, drain, 0)
-    for flow in range(4):
-        across(flow, 15).wait()
-    for flow in (0, 2):
-        forward(flow, 15).wait_send()
-        across(flow, 0).wait()
-        across(flow, 16).wait()
+    for copy in crossing:
+        copy.wait_recv()
+    for copy in sent:
+        copy.wait_send()
 
 
 def gather(queries, keys, values, d_out):
-    whole = jax.ShapeDtypeStruct((XHI, YN, 32, 128, HD), jnp.bfloat16)
+    whole = jax.ShapeDtypeStruct(WHOLE, jnp.bfloat16)
     part = jax.ShapeDtypeStruct((PIECES, HALF, GROUP * HD), jnp.bfloat16)
     dma = pltpu.SemaphoreType.DMA
     return pl.pallas_call(
@@ -226,7 +274,8 @@
         out_specs=(ANY,) * 4,
         scratch_shapes=[
             dma((2, YN)), dma((2, YN)), dma((2, PIECES)), dma((2, PIECES)),
-            dma((4, 17)), dma((4, 17)), dma((4, 17)), dma((4, 17)), dma((4,)),
+            dma((4,)), dma((4,)), dma((2, 5, 2)), dma((2, 5, 2)), dma((2, 5)), dma((2, 5)),
+            dma((2, 2, ZN)), dma((2, 2, ZN)), dma((23,)), dma((23,)), dma((4,)),
         ],
         compiler_params=pltpu.CompilerParams(collective_id=0, has_side_effects=True),
         name="gather",
@@ -427,51 +476,168 @@
 
 def scatter_kernel(
     o_ref, dq_ref, dk_ref, dv_ref, ao_ref, gq_ref, gk_ref, gv_ref,
-    own, part, recv, done,
-    own_sem, c_send, c_recv, r_send, r_recv, p_send, p_recv, y_send, y_recv, local,
+    own, part, kz_in, kx_half, kx_in, vx_half, vx_in, vz_in,
+    own_sem, c_send, c_recv, kz_send, kz_recv, kx_send, kx_recv, vx_send, vx_recv,
+    vz_send, vz_recv, p_send, p_recv, y_send, y_recv, local,
 ):
     at = Spot()
     greet(at.peers())
     ours = [dk_ref, dv_ref]
-
-    def target(flow, step):
-        ring = flow // 2
-        if flow % 2 == 0:
-            return lax.rem(at.number[ring] + 17 - step, RING)
-        return lax.rem(at.number[ring] + 16 + step, RING)
-
-    def load(flow, step, n):
-        piece = at.chunk(ours[flow // 2], flow // 2, n, at.core)
-        return pltpu.make_async_copy(piece, own.at[flow, step], own_sem.at[flow, step])
-
-    def across(flow, step, n):
-        piece = at.chunk(ours[flow // 2], flow // 2, n, 1 - at.core)
-        return remote(
-            piece, part.at[flow, step], c_send.at[flow, step], c_recv.at[flow, step], at.partner
+    sent, moves = [], []
+
+    def go(src, dst, send, recv, peer):
+        copy = remote(src, dst, send, recv, peer)
+        copy.start()
+        sent.append(copy)
+        return copy
+
+    waiting = {}
+    for dz in (4, 3, -3, 2, -2, 1, -1, 0):
+        for number in range(2):
+            place = (number, dz + 3)
+            load = pltpu.make_async_copy(
+                at.across_x(ours[number], at.core, dz), own.at[place], own_sem.at[place]
+            )
+            load.start()
+            theirs = go(
+                at.across_x(ours[number], 1 - at.core, dz),
+                part.at[place],
+                c_send.at[place],
+                c_recv.at[place],
+                at.partner,
+            )
+            waiting[number, dz] = (load, theirs)
+
+    def f32(value):
+        return value.astype(jnp.float32)
+
+    def joined(number, dz):
+        load, theirs = waiting[number, dz]
+        load.wait()
+        theirs.wait_recv()
+        place = (number, dz + 3)
+        for xh in range(XHI):
+            total = f32(own[(*place, xh)]) + f32(part[(*place, xh)])
+            own[(*place, xh)] = total.astype(jnp.bfloat16)
+
+    def add(place, value):
+        own[place] = (f32(own[place]) + f32(value)).astype(jnp.bfloat16)
+
+    def kz(step, half, way):
+        dz = (5 - step) if way == 0 else (step - 5)
+        dz = 4 if dz == -4 else dz
+        place = (way, step - 1, half)
+        return go(
+            own.at[0, dz + 3, :, halves(half)],
+            kz_in.at[place],
+            kz_send.at[place],
+            kz_recv.at[place],
+            at.z_peer[way],
         )
 
-    def forward(flow, step):
-        return remote(
-            own.at[flow, step],
-            recv.at[flow, step - 1],
-            r_send.at[flow, step - 1],
-            r_recv.at[flow, step - 1],
-            at.next[flow],
-        )
-
-    def begin(step, carry):
-        for flow in range(4):
-            load(flow, step, target(flow, step)).start()
-            across(flow, step, target(flow, step)).start()
-        return carry
-
-    lax.fori_loop(1, 16, begin, 0)
-    for flow in (0, 2):
-        load(flow, 16, target(flow, 16)).start()
-        across(flow, 16, target(flow, 16)).start()
-        load(flow, 0, at.number[flow // 2]).start()
-        across(flow, 0, at.number[flow // 2]).start()
-    moves = []
+    def kz_step(before, step):
+        after = {}
+        for way in range(2):
+            dz = (5 - step) if way == 0 else (step - 5)
+            joined(0, dz)
+            for half in range(2):
+                if (half, way) in before:
+                    before[half, way].wait_recv()
+                    add((0, dz + 3, slice(None), halves(half)), kz_in[way, step - 2, half])
+                after[half, way] = kz(step, half, way)
+        return after
+
+    def edge(dx):
+        x = at.x_at(dx)
+        return x // 2, lax.rem(x, 2)
+
+    def own_chunk(number, dz, dx, half=None):
+        xh, xl = edge(dx)
+        return (number, dz + 3, xh, halves(half), xl)
+
+    def x_first(number, dz, inbox, send, recv):
+        out = []
+        for way in range(2):
+            place = (dz + 3, way) if number else (way,)
+            sem = (0, *place)
+            out.append(
+                go(
+                    own.at[own_chunk(number, dz, 2, way)],
+                    inbox.at[place],
+                    send.at[sem],
+                    recv.at[sem],
+                    at.x_peer[way],
+                )
+            )
+        return out
+
+    def x_second(number, dz, first, half_box, inbox, send, recv):
+        out = []
+        for way in range(2):
+            place = (dz + 3, way) if number else (way,)
+            sem = (1, *place)
+            dx = 1 - 2 * way
+            first[way].wait_recv()
+            add(own_chunk(number, dz, dx, way), half_box[place])
+            out.append(
+                go(
+                    own.at[own_chunk(number, dz, dx)],
+                    inbox.at[place],
+                    send.at[sem],
+                    recv.at[sem],
+                    at.x_peer[way],
+                )
+            )
+        return out
+
+    def x_third(number, dz, second, inbox):
+        for way in range(2):
+            place = (dz + 3, way) if number else (way,)
+            second[way].wait_recv()
+        places = [(dz + 3, way) if number else (way,) for way in range(2)]
+        mine = own_chunk(number, dz, 0)
+        total = f32(own[mine]) + f32(inbox[places[0]]) + f32(inbox[places[1]])
+        own[mine] = total.astype(jnp.bfloat16)
+
+    v_first, v_second = {}, {}
+
+    def va(dz):
+        joined(1, dz)
+        v_first[dz] = x_first(1, dz, vx_half, vx_send, vx_recv)
+
+    def vb(dz):
+        v_second[dz] = x_second(1, dz, v_first[dz], vx_half, vx_in, vx_send, vx_recv)
+
+    def vc(dz):
+        x_third(1, dz, v_second[dz], vx_in)
+
+    v_step = [None, None]
+
+    def vz(step):
+        for way in range(2):
+            dz = (5 - step) if way == 0 else (step - 5)
+            dz = 4 if dz == -4 else dz
+            half = way if step == 1 else None
+            if step == 2:
+                v_step[way].wait_recv()
+                add(own_chunk(1, dz, 0, way), vz_in[way, 0, halves(way)])
+            elif step > 2:
+                v_step[way].wait_recv()
+                add(own_chunk(1, dz, 0), vz_in[way, step - 2])
+            place = (way, step - 1)
+            v_step[way] = go(
+                own.at[own_chunk(1, dz, 0, half)],
+                vz_in.at[(*place, halves(half))],
+                vz_send.at[place],
+                vz_recv.at[place],
+                at.z_peer[way],
+            )
+
+    joined(0, 4)
+    k_step = {(way, way): kz(1, way, way) for way in range(2)}
+    va(4)
+    va(3)
+    va(-3)
     for number, (src, dst) in enumerate([(o_ref, ao_ref), (dq_ref, gq_ref)]):
         for place, (dx, dy) in enumerate(at.offsets):
             xh, y = at.part_of(dx, dy)
@@ -491,50 +657,46 @@
                 )
             move.start()
             moves.append(move)
-
-    def wide(ref, flow, step):
-        return ref[flow, step].astype(jnp.float32)
-
-    def ready(flow, step, n):
-        load(flow, step, n).wait()
-        across(flow, step, n).wait_recv()
-
-    def send(flow, step, first):
-        ready(flow, step, target(flow, step))
-        total = wide(own, flow, step) + wide(part, flow, step)
-        if not first:
-            forward(flow, step - 1).wait_recv()
-            total = total + wide(recv, flow, step - 2)
-        own[flow, step] = total.astype(jnp.bfloat16)
-        forward(flow, step).start()
-
-    for flow in range(4):
-        send(flow, 1, True)
-
-    def step_body(step, carry):
-        for flow in range(4):
-            send(flow, step, False)
-        return carry
-
-    lax.fori_loop(2, 16, step_body, 0)
-    for flow in (0, 2):
-        send(flow, 16, False)
-    for number, flow in enumerate((0, 2)):
-        ready(flow, 0, at.number[number])
-        total = wide(own, flow, 0) + wide(part, flow, 0)
-        forward(flow, 16).wait_recv()
-        forward(flow + 1, 15).wait_recv()
-        total = total + wide(recv, flow, 15) + wide(recv, flow + 1, 14)
-        done[number] = total.astype(jnp.bfloat16)
-        dst = (gk_ref, gv_ref)[number]
+    vb(4)
+    va(2)
+    va(-2)
+    k_step = kz_step(k_step, 2)
+    vb(3)
+    vb(-3)
+    vc(4)
+    vz(1)
+    va(1)
+    va(-1)
+    vb(2)
+    vb(-2)
+    vc(3)
+    vc(-3)
+    vz(2)
+    va(0)
+    k_step = kz_step(k_step, 3)
+    vb(1)
+    vb(-1)
+    vc(2)
+    vc(-2)
+    vz(3)
+    vb(0)
+    vc(1)
+    vc(-1)
+    vz(4)
+    k_step = kz_step(k_step, 4)
+    vc(0)
+
+    def finish(number, ref):
         for dy in range(YN):
             _, y = at.part_of(0, dy)
-            slot = dst.at[:, lanes(at.y, HD)]
+            xh, xl = edge(0)
+            piece = own.at[number, 3, xh, y, xl]
+            slot = ref.at[:, lanes(at.y, HD)]
             if dy == 0:
-                move = pltpu.make_async_copy(done.at[number, y], slot, local.at[2 + number])
+                move = pltpu.make_async_copy(piece, slot, local.at[2 + number])
             else:
                 move = remote(
-                    done.at[number, y],
+                    piece,
                     slot,
                     y_send.at[number, dy],
                     y_recv.at[number, dy],
@@ -542,50 +704,61 @@
                 )
             move.start()
             moves.append(move)
+
+    joined(0, 0)
+    for half in range(2):
+        for way in range(2):
+            k_step[half, way].wait_recv()
+        where = (0, 3, slice(None), halves(half))
+        total = f32(own[where]) + f32(kz_in[0, 3, half]) + f32(kz_in[1, 3, half])
+        own[where] = total.astype(jnp.bfloat16)
+    first = x_first(0, 0, kx_half, kx_send, kx_recv)
+    for way in range(2):
+        v_step[way].wait_recv()
+    mine = own_chunk(1, 0, 0)
+    total = f32(own[mine]) + f32(vz_in[0, 3]) + f32(vz_in[1, 3])
+    own[mine] = total.astype(jnp.bfloat16)
+    finish(1, gv_ref)
+    second = x_second(0, 0, first, kx_half, kx_in, kx_send, kx_recv)
+    x_third(0, 0, second, kx_in)
+    finish(0, gk_ref)
     for move in moves:
         move.wait()
-
-    def drain(step, carry):
-        for flow in range(4):
-            forward(flow, step).wait_send()
-            across(flow, step, target(flow, step)).wait_send()
-        return carry
-
-    lax.fori_loop(1, 16, drain, 0)
-    for flow in (0, 2):
-        forward(flow, 16).wait_send()
-        across(flow, 16, target(flow, 16)).wait_send()
-        across(flow, 0, at.number[flow // 2]).wait_send()
+    for copy in sent:
+        copy.wait_send()
 
 
 def scatter(out, dq, dk, dv):
     tokens = jax.ShapeDtypeStruct((128, QH * HD), jnp.bfloat16)
     pairs = jax.ShapeDtypeStruct((128, KVH * HD), jnp.bfloat16)
     dma = pltpu.SemaphoreType.DMA
-    slots = (YN, 128, HD)
+
+    def box(*shape):
+        return pltpu.VMEM((*shape, 128, HD), jnp.bfloat16)
+
     return pl.pallas_call(
         scatter_kernel,
         out_shape=(tokens, tokens, pairs, pairs),
         in_specs=[ANY] * 4,
         out_specs=(ANY,) * 4,
         scratch_shapes=[
-            pltpu.VMEM((4, 17) + slots, jnp.bfloat16),
-            pltpu.VMEM((4, 17) + slots, jnp.bfloat16),
-            pltpu.VMEM((4, 16) + slots, jnp.bfloat16),
-            pltpu.VMEM((2,) + slots, jnp.bfloat16),
-            dma((4, 17)), dma((4, 17)), dma((4, 17)), dma((4, 16)), dma((4, 16)),
+            box(2, ZN, XHI, YN, XLO),
+            box(2, ZN, XHI, YN, XLO),
+            box(2, 4, 2, XHI, 2, XLO),
+            box(2, 2),
+            box(2, YN),
+            box(ZN, 2, 2),
+            box(ZN, 2, YN),
+            box(2, 4, YN),
+            dma((2, ZN)), dma((2, ZN)), dma((2, ZN)), dma((2, 4, 2)), dma((2, 4, 2)),
+            dma((2, 2)), dma((2, 2)), dma((2, ZN, 2)), dma((2, ZN, 2)), dma((2, 4)), dma((2, 4)),
             dma((2, PIECES)), dma((2, PIECES)), dma((2, YN)), dma((2, YN)), dma((4,)),
         ],
         compiler_params=pltpu.CompilerParams(
             collective_id=1, has_side_effects=True, vmem_limit_bytes=48 << 20
         ),
         name="scatter",
-    )(
-        out,
-        dq,
-        dk.reshape(XHI, YN, 32, 128, HD),
-        dv.reshape(XHI, YN, 32, 128, HD),
-    )
+    )(out, dq, dk.reshape(WHOLE), dv.reshape(WHOLE))
 
 
 def shards(queries, keys, values, d_out, lengths):

time: 299 us -> 258 us (0.86)
  Pallas kernels: 288 us -> 248 us
    pallas_call x1, Pallas kernels: 111 us -> 85.7 us  [scatter(): pl.pallas_call(scatter_kernel, out_shape=(tokens, tokens, pairs, pairs),...]
    pallas_call x1, Pallas kernels: 109 us -> 84.5 us  [gather(): pl.pallas_call(gather_kernel, out_shape=(whole, whole, part, part), in_sp...]
    pallas_call x1, Pallas kernels: 67.7 us -> 78.1 us  [attention(): pl.pallas_call(attention_kernel, out_shape=(part_shape, part_shape, whole...]
where the time goes in v1:
time: 258 us
  Pallas kernels  248 us (96%)
  local copies, waits for them, and re-layouts  6.4 us (2%)
    pallas_call x1, Pallas kernels, scatter(): pl.pallas_call(scatter_kernel, out_shape=(tokens, tokens, pairs, pairs),...  85.7 us
    pallas_call x1, Pallas kernels, gather(): pl.pallas_call(gather_kernel, out_shape=(whole, whole, part, part), in_sp...  84.5 us
    pallas_call x1, Pallas kernels, attention(): pl.pallas_call(attention_kernel, out_shape=(part_shape, part_shape, whole...  78.1 us

profile of v1, /device:TPU:2, one launch (start us, length us, event | category | flops | bytes accessed | tf_op | source)
XLA Modules:
  0.0 258.0 jit_solution(6028961851551419451)
XLA Ops:
  0.7 0.1 iota_add_fusion
  0.8 0.7 copy.11
  1.5 0.1 reduce-window.8
  1.6 0.1 reduce
  1.7 0.8 select_reduce_fusion
  2.4 0.1 slice_reduce_fusion
  2.6 0.1 fusion.17
  2.7 0.5 convert_element_type.3.touched
  3.2 0.7 pad_add_fusion.meta
  3.9 0.7 tile.9.start_ref
  4.6 84.5 %gather.1 = (bf16[2,4,2,8,2,128,128]{6,5,4,3,2,1,0:T(8,128)(2,1)}, bf16[2,4,2,8,2,128,128]{6,5,4,3,2,1,0:T(8,128)(2,1)}, bf16[8,64,512]{2,1,0:T(8,128)(2,1)}, bf16[8,64,512]{2,1,0:T(8,128)(2,1)}) custom-call(bf16[128,2048]{1,0:T(8,128)(2,1)} %q_ref.1, bf16[128,512]{1,0:T(8,128)(2,1)} %k_ref.1, bf16[128,512]{1,0:T(8,128)(2,1)} %v_ref.1, bf16[128,2048]{1,0:T(8,128)(2,1)} %g_ref.1), custom_call_target="tpu_custom_call" | custom-call | tf_op jit(solution)/shard_map/gather/pallas_call | solution.py:270
  89.1 78.1 %attention.1 = (bf16[8,64,512]{2,1,0:T(8,128)(2,1)}, bf16[8,64,512]{2,1,0:T(8,128)(2,1)}, bf16[32768,128]{1,0:T(8,128)(2,1)}, bf16[32768,128]{1,0:T(8,128)(2,1)}) custom-call(s32[8,3]{1,0:T(8,128)} %pad_add_fusion.meta, s32[64]{0:T(128)} %convert_element_type.3.touched, s32[8,1,256]{2,1,0:T(1,128)} %tile.9.start_ref, ...), custom_call_target="tpu_custom_call" | custom-call | tf_op jit(solution)/shard_map/attention/pallas_call | solution.py:447
  167.2 0.0 copy-start
  167.2 1.0 copy-done
  168.3 0.0 copy-start.1
  168.3 1.0 copy-done.1
  169.3 85.7 %scatter.1 = (bf16[128,2048]{1,0:T(8,128)(2,1)S(1)}, bf16[128,2048]{1,0:T(8,128)(2,1)S(1)}, bf16[128,512]{1,0:T(8,128)(2,1)S(1)}, bf16[128,512]{1,0:T(8,128)(2,1)S(1)}) custom-call(bf16[8,64,512]{2,1,0:T(8,128)(2,1)S(1)} %copy-done, bf16[8,64,512]{2,1,0:T(8,128)(2,1)S(1)} %copy-done.1, bf16[2,4,2,8,2,128,128]{6,5,4,3,2,1,0:T(8,128)(2,1)} %bitcast.5, ...), custom_call_target="tpu_custom_call" | custom-call | tf_op jit(solution)/shard_map/scatter/pallas_call | solution.py:739
  255.1 0.8 copy.16
  255.9 0.8 copy.17
  256.6 0.7 copy.18
  257.3 0.7 copy.19
  (3 shorter events, 0.0 us)
Async XLA Ops:
  167.2 1.0 copy-start
  168.3 1.0 copy-start.1

commit v2 on v1

--- a/solution.py
+++ b/solution.py
@@ -22,8 +22,10 @@
 PIECES = XHI * YN
 ROWS = GROUP * HALF
 KB = 512
+UNITS = 4
 KBLOCKS = SEQ // KB
-SPAN = DOC_MOST // KB + 2
+SPAN = (DOC_MOST + HALF - 1 + KB - 1) // KB
+FLUSH_SLOTS = 4
 
 MESH = pl.DeviceIdType.MESH
 ANY = pl.BlockSpec(memory_space=pl.ANY)
@@ -110,7 +112,7 @@
     at = Spot()
     greet(at.peers())
     copies = []
-    for number, (src, dst) in enumerate([(v_ref, va_ref), (k_ref, ka_ref)]):
+    for number, (src, dst) in enumerate([(k_ref, ka_ref), (v_ref, va_ref)]):
         slot = dst.at[at.xh, at.y, at.core, at.z, at.xl]
         keep = pltpu.make_async_copy(src.at[:, lanes(at.y, HD)], slot, local.at[number])
         keep.start()
@@ -189,35 +191,15 @@
 
     for copy in copies[0]:
         copy.wait()
-    v_step = [vz(1, way) for way in range(2)]
-    vx_start(0)
+    k_first = [kx(way, at.chunk(ka_ref, 0, 0), way) for way in range(2)]
     for copy in copies[1]:
         copy.wait()
-    k_first = [kx(way, at.chunk(ka_ref, 0, 0), way) for way in range(2)]
-
-    moves = []
-    for number, (src, dst) in enumerate([(q_ref, qi_ref), (g_ref, gi_ref)]):
-        for place, (dx, dy) in enumerate(at.offsets):
-            xh, y = at.part_of(dx, dy)
-            piece = src.at[pl.ds(pl.multiple_of(xh * HALF, HALF), HALF), lanes(y, GROUP * HD)]
-            slot = dst.at[at.xh * YN + at.y]
-            if place == 0:
-                move = pltpu.make_async_copy(piece, slot, local.at[2 + number])
-            else:
-                move = remote(
-                    piece,
-                    slot,
-                    p_send.at[number, place],
-                    p_recv.at[number, place],
-                    at.part_device(dx, dy),
-                )
-            move.start()
-            moves.append(move)
-
+    v_step = [vz(1, way) for way in range(2)]
     k_second = []
     for way in range(2):
         k_first[way].wait_recv()
         k_second.append(kx(2 + way, at.chunk(ka_ref, 2 * way - 1, 0, way), way))
+    vx_start(0)
 
     def vz_next(step):
         for way in range(2):
@@ -245,6 +227,25 @@
     vx_end(-1)
     vx_end(1)
     k_step = kz_step(k_step, 3)
+    moves = []
+    for number, (src, dst) in enumerate([(q_ref, qi_ref), (g_ref, gi_ref)]):
+        for place, (dx, dy) in enumerate(at.offsets):
+            xh, y = at.part_of(dx, dy)
+            piece = src.at[pl.ds(pl.multiple_of(xh * HALF, HALF), HALF), lanes(y, GROUP * HD)]
+            slot = dst.at[at.xh * YN + at.y]
+            if place == 0:
+                move = pltpu.make_async_copy(piece, slot, local.at[2 + number])
+            else:
+                move = remote(
+                    piece,
+                    slot,
+                    p_send.at[number, place],
+                    p_recv.at[number, place],
+                    at.part_device(dx, dy),
+                )
+            move.start()
+            moves.append(move)
+
     vx_forward(-3)
     vx_forward(3)
     vx_end(-2)
@@ -283,20 +284,24 @@
 
 
 def attention_kernel(
-    meta, touched, start_ref, q_ref, g_ref, ka_ref, va_ref, o_ref, dq_ref, dk_ref, dv_ref,
-    kbuf, vbuf, sbuf, pbuf, dk_acc, dv_acc, flush, k_sem, v_sem, f_sem,
+    meta, first_use, last_use, start_ref, q_ref, g_ref, ka_ref, va_ref, o_ref, dq_ref, dk_ref,
+    dv_ref, kbuf, vbuf, sbuf, pbuf, dk_acc, dv_acc, flush, zeros, pending, k_sem, v_sem, f_sem,
+    z_sem,
 ):
     scaling = HD ** (-0.5)
     factor = scaling * math.log2(math.e)
 
-    def rows_of(j):
-        return pl.ds(pl.multiple_of(j * KB, KB), KB)
+    def block(j, size=KB):
+        return pl.ds(pl.multiple_of(j * KB, KB), size)
+
+    def span(low, j, size=KB):
+        return pl.ds(pl.multiple_of(low + j * KB, HALF), size)
 
     def fetches(i, slot, j):
-        src = rows_of(meta[i, 0] + j)
+        src = span(meta[i, 0], j)
         return (
-            pltpu.make_async_copy(ka_ref.at[src], kbuf.at[slot, rows_of(j)], k_sem.at[slot, j]),
-            pltpu.make_async_copy(va_ref.at[src], vbuf.at[slot, rows_of(j)], v_sem.at[slot, j]),
+            pltpu.make_async_copy(ka_ref.at[src], kbuf.at[slot, block(j)], k_sem.at[slot, j]),
+            pltpu.make_async_copy(va_ref.at[src], vbuf.at[slot, block(j)], v_sem.at[slot, j]),
         )
 
     def fetch(i, slot):
@@ -318,44 +323,96 @@
             a, b, (((da,), (db,)), ((), ())), preferred_element_type=jnp.float32
         )
 
+    def in_pairs(count, body, carry):
+        carry = lax.fori_loop(
+            0, count // UNITS, lambda j, c: body(UNITS * j, UNITS * KB, c), carry
+        )
+        done, units = count // UNITS * UNITS, UNITS // 2
+        while units:
+            more = lax.rem(count // units, 2)
+            carry = lax.cond(
+                more == 1,
+                lambda c, done=done, units=units: body(done, units * KB, c),
+                lambda c: c,
+                carry,
+            )
+            done, units = done + more * units, units // 2
+        return carry
+
+    def blanks(kb):
+        return (
+            pltpu.make_async_copy(zeros, dk_ref.at[block(kb)], z_sem.at[0, kb]),
+            pltpu.make_async_copy(zeros, dv_ref.at[block(kb)], z_sem.at[1, kb]),
+        )
+
+    def flushes(kb, slot):
+        return (
+            pltpu.make_async_copy(flush.at[0, slot], dk_ref.at[block(kb)], f_sem.at[0, slot]),
+            pltpu.make_async_copy(flush.at[1, slot], dv_ref.at[block(kb)], f_sem.at[1, slot]),
+        )
+
     fetch(0, 0)
-
-    def piece(i, seen):
+    zeros[...] = jnp.zeros((KB, HD), jnp.bfloat16)
+    for slot in range(FLUSH_SLOTS):
+        pending[slot] = 0
+
+    def blank_start(kb, carry):
+        @pl.when(first_use[kb] < 0)
+        def _():
+            for copy in blanks(kb):
+                copy.start()
+
+        return carry
+
+    lax.fori_loop(0, KBLOCKS, blank_start, 0)
+
+    def piece(i, carry):
         slot = lax.rem(i, 2)
 
         @pl.when(i + 1 < PIECES)
         def _():
             fetch(i + 1, 1 - slot)
 
-        low, count, first = meta[i, 0], meta[i, 1], meta[i, 2]
+        low, count, first, last_start = meta[i, 0], meta[i, 1], meta[i, 2], meta[i, 3]
         q = stacked(q_ref[i])
         g = stacked(g_ref[i])
         starts = start_ref[i]
         times = first + lax.rem(lax.broadcasted_iota(jnp.int32, (1, ROWS), 1), HALF)
-        key_iota = lax.broadcasted_iota(jnp.int32, (KB, ROWS), 0)
-
-        def scores_step(j, top):
-            fetches(i, slot, j)[0].wait()
-            s = mm(kbuf[slot, rows_of(j)], q, 1, 1)
-            base = (low + j) * KB
-            s = jnp.where((key_iota >= starts - base) & (key_iota <= times - base), s, NEG_FILL)
-            sbuf[rows_of(j)] = s
-            return jnp.maximum(top, jnp.max(s.reshape(KB // 8, 8, ROWS), axis=0))
-
-        top = lax.fori_loop(0, count, scores_step, jnp.full((8, ROWS), NEG_FILL, jnp.float32))
+
+        def scores_step(j, size, top):
+            for part in range(size // KB):
+                fetches(i, slot, j + part)[0].wait()
+            base = low + j * KB
+
+            def finish(s):
+                sbuf[block(j, size)] = s
+                return jnp.maximum(top, jnp.max(s.reshape(size // 8, 8, ROWS), axis=0))
+
+            def scores():
+                return mm(kbuf[slot, block(j, size)], q, 1, 1)
+
+            def masked():
+                key = lax.broadcasted_iota(jnp.int32, (size, ROWS), 0)
+                seen = (key >= starts - base) & (key <= times - base)
+                return finish(jnp.where(seen, scores(), NEG_FILL))
+
+            whole = (base >= last_start) & (base + size - 1 <= first)
+            return lax.cond(whole, lambda: finish(scores()), masked)
+
+        top = in_pairs(count, scores_step, jnp.full((8, ROWS), NEG_FILL, jnp.float32))
         top = jnp.max(top, axis=0, keepdims=True)
 
-        def weights_step(j, carry):
+        def weights_step(j, size, carry):
             total, out = carry
-            fetches(i, slot, j)[1].wait()
-            p = jnp.exp2((sbuf[rows_of(j)] - top) * factor)
-            total = total + jnp.sum(p.reshape(KB // 8, 8, ROWS), axis=0)
+            for part in range(size // KB):
+                fetches(i, slot, j + part)[1].wait()
+            p = jnp.exp2((sbuf[block(j, size)] - top) * factor)
+            total = total + jnp.sum(p.reshape(size // 8, 8, ROWS), axis=0)
             p = p.astype(jnp.bfloat16)
-            pbuf[rows_of(j)] = p
-            return total, out + mm(vbuf[slot, rows_of(j)], p, 0, 0)
-
-        total, out = lax.fori_loop(
-            0,
+            pbuf[block(j, size)] = p
+            return total, out + mm(vbuf[slot, block(j, size)], p, 0, 0)
+
+        total, out = in_pairs(
             count,
             weights_step,
             (jnp.zeros((8, ROWS), jnp.float32), jnp.zeros((HD, ROWS), jnp.float32)),
@@ -365,81 +422,91 @@
         o_ref[i] = unstacked(out.T.astype(jnp.bfloat16))
         g_turned = g.astype(jnp.float32).T
         delta = jnp.sum(g_turned * out, axis=0, keepdims=True) * inverse
-        g_turned = g_turned * inverse
-        g_rows = g_turned.T.astype(jnp.bfloat16)
+        g_rows = (g_turned * inverse).T.astype(jnp.bfloat16)
+        block_low, block_end = low // KB, (low + count * KB - 1) // KB + 1
 
         def clear(kb, carry):
-            dk_acc[rows_of(kb)] = jnp.zeros((KB, HD), jnp.float32)
-            dv_acc[rows_of(kb)] = jnp.zeros((KB, HD), jnp.float32)
+            @pl.when(first_use[kb] == i)
+            def _():
+                dk_acc[block(kb)] = jnp.zeros((KB, HD), jnp.float32)
+                dv_acc[block(kb)] = jnp.zeros((KB, HD), jnp.float32)
+
             return carry
 
-        lax.fori_loop(jnp.maximum(low, seen), low + count, clear, 0)
-
-        def grad_step(j, dq):
-            k = kbuf[slot, rows_of(j)]
-            p = pbuf[rows_of(j)]
-            gp = mm(vbuf[slot, rows_of(j)], g_rows, 1, 1)
+        lax.fori_loop(block_low, block_end, clear, 0)
+
+        def grad_step(j, size, dq):
+            k = kbuf[slot, block(j, size)]
+            p = pbuf[block(j, size)]
+            gp = mm(vbuf[slot, block(j, size)], g_rows, 1, 1)
             ds = (p.astype(jnp.float32) * (gp - delta)).astype(jnp.bfloat16)
-            where = rows_of(low + j)
+            where = span(low, j, size)
             dv_acc[where] += mm(p, g_rows, 1, 0)
             dk_acc[where] += mm(ds, q, 1, 0)
             return dq + mm(k, ds, 0, 0)
 
-        dq = lax.fori_loop(0, count, grad_step, jnp.zeros((HD, ROWS), jnp.float32))
+        dq = in_pairs(count, grad_step, jnp.zeros((HD, ROWS), jnp.float32))
         dq_ref[i] = unstacked((dq * scaling).T.astype(jnp.bfloat16))
-        return low + count
+
+        def flush_step(kb, carry):
+            @pl.when(last_use[kb] == i)
+            def _():
+                slot = lax.rem(kb, FLUSH_SLOTS)
+
+                @pl.when(pending[slot] > 0)
+                def _():
+                    for copy in flushes(kb, slot):
+                        copy.wait()
+
+                pending[slot] = 1
+                flush[0, slot] = (dk_acc[block(kb)] * scaling).astype(jnp.bfloat16)
+                flush[1, slot] = dv_acc[block(kb)].astype(jnp.bfloat16)
+                for copy in flushes(kb, slot):
+                    copy.start()
+
+            return carry
+
+        lax.fori_loop(block_low, block_end, flush_step, 0)
+        return carry
 
     lax.fori_loop(0, PIECES, piece, 0)
-
-    def flushes(kb, slot):
-        return (
-            pltpu.make_async_copy(flush.at[0, slot], dk_ref.at[rows_of(kb)], f_sem.at[0, slot]),
-            pltpu.make_async_copy(flush.at[1, slot], dv_ref.at[rows_of(kb)], f_sem.at[1, slot]),
-        )
-
-    def flush_step(kb, carry):
-        slot = lax.rem(kb, 2)
-
-        @pl.when(kb >= 2)
+    for slot in range(FLUSH_SLOTS):
+
+        @pl.when(pending[slot] > 0)
         def _():
-            for copy in flushes(kb - 2, slot):
+            for copy in flushes(0, slot):
                 copy.wait()
 
-        @pl.when(touched[kb] > 0)
+    def blank_wait(kb, carry):
+        @pl.when(first_use[kb] < 0)
         def _():
-            flush[0, slot] = (dk_acc[rows_of(kb)] * scaling).astype(jnp.bfloat16)
-            flush[1, slot] = dv_acc[rows_of(kb)].astype(jnp.bfloat16)
-
-        @pl.when(touched[kb] == 0)
-        def _():
-            flush[0, slot] = jnp.zeros((KB, HD), jnp.bfloat16)
-            flush[1, slot] = jnp.zeros((KB, HD), jnp.bfloat16)
-
-        for copy in flushes(kb, slot):
-            copy.start()
+            for copy in blanks(kb):
+                copy.wait()
+
         return carry
 
-    lax.fori_loop(0, KBLOCKS, flush_step, 0)
-    for kb in (KBLOCKS - 2, KBLOCKS - 1):
-        for copy in flushes(kb, kb % 2):
-            copy.wait()
+    lax.fori_loop(0, KBLOCKS, blank_wait, 0)
 
 
 def attention(lengths, q, g, keys, values):
     x, y, z, core = here()
     ends = jnp.cumsum(lengths)
     part = jnp.arange(PIECES, dtype=jnp.int32)
-    block = (part // YN) * 128 + lax.rem(part, YN) * 32 + core * 16 + z * 2 + lax.rem(x, 2)
-    first = block * 128 + (x // 2) * HALF
+    tile = (part // YN) * 128 + lax.rem(part, YN) * 32 + core * 16 + z * 2 + lax.rem(x, 2)
+    first = tile * 128 + (x // 2) * HALF
     times = first[:, None] + jnp.arange(HALF, dtype=jnp.int32)[None, :]
     starts = jnp.sum(
         jnp.where(ends[None, None, :] <= times[:, :, None], lengths[None, None, :], 0), axis=2
     )
-    low = starts[:, 0] // KB
-    high = (first + HALF - 1) // KB
-    meta = jnp.stack([low, high - low + 1, first], axis=1).astype(jnp.int32)
-    block_ids = jnp.arange(KBLOCKS, dtype=jnp.int32)[:, None]
-    touched = jnp.any((block_ids >= low[None]) & (block_ids <= high[None]), axis=1)
+    end = first + HALF
+    count = (end - starts[:, 0] + KB - 1) // KB
+    low = jnp.maximum(end - count * KB, 0)
+    meta = jnp.stack([low, count, first, starts[:, HALF - 1]], axis=1).astype(jnp.int32)
+    ids = jnp.arange(KBLOCKS, dtype=jnp.int32)[:, None]
+    used = (ids >= low[None] // KB) & (ids <= (low + count * KB - 1)[None] // KB)
+    last_use = jnp.max(jnp.where(used, part[None], -1), axis=1)
+    first_use = jnp.min(jnp.where(used, part[None], PIECES), axis=1)
+    first_use = jnp.where(last_use < 0, -1, first_use)
     start_rows = jnp.tile(starts, (1, GROUP)).reshape(PIECES, 1, ROWS).astype(jnp.int32)
     part_shape = jax.ShapeDtypeStruct((PIECES, HALF, GROUP * HD), jnp.bfloat16)
     whole = jax.ShapeDtypeStruct((SEQ, HD), jnp.bfloat16)
@@ -447,7 +514,7 @@
     return pl.pallas_call(
         attention_kernel,
         out_shape=(part_shape, part_shape, whole, whole),
-        in_specs=[SMEM, SMEM, VMEM, VMEM, VMEM, ANY, ANY],
+        in_specs=[SMEM, SMEM, SMEM, VMEM, VMEM, VMEM, ANY, ANY],
         out_specs=(VMEM, VMEM, ANY, ANY),
         scratch_shapes=[
             pltpu.VMEM((2, SPAN * KB, HD), jnp.bfloat16),
@@ -456,16 +523,20 @@
             pltpu.VMEM((SPAN * KB, ROWS), jnp.bfloat16),
             pltpu.VMEM((SEQ, HD), jnp.float32),
             pltpu.VMEM((SEQ, HD), jnp.float32),
-            pltpu.VMEM((2, 2, KB, HD), jnp.bfloat16),
+            pltpu.VMEM((2, FLUSH_SLOTS, KB, HD), jnp.bfloat16),
+            pltpu.VMEM((KB, HD), jnp.bfloat16),
+            pltpu.SMEM((FLUSH_SLOTS,), jnp.int32),
             dma((2, SPAN)),
             dma((2, SPAN)),
-            dma((2, 2)),
+            dma((2, FLUSH_SLOTS)),
+            dma((2, KBLOCKS)),
         ],
         compiler_params=pltpu.CompilerParams(vmem_limit_bytes=62 << 20),
         name="attention",
     )(
         meta,
-        touched.astype(jnp.int32),
+        first_use.astype(jnp.int32),
+        last_use.astype(jnp.int32),
         start_rows,
         q,
         g,
@@ -638,25 +709,6 @@
     va(4)
     va(3)
     va(-3)
-    for number, (src, dst) in enumerate([(o_ref, ao_ref), (dq_ref, gq_ref)]):
-        for place, (dx, dy) in enumerate(at.offsets):
-            xh, y = at.part_of(dx, dy)
-            piece = src.at[xh * YN + y]
-            slot = dst.at[
-                pl.ds(pl.multiple_of(at.xh * HALF, HALF), HALF), lanes(at.y, GROUP * HD)
-            ]
-            if place == 0:
-                move = pltpu.make_async_copy(piece, slot, local.at[number])
-            else:
-                move = remote(
-                    piece,
-                    slot,
-                    p_send.at[number, place],
-                    p_recv.at[number, place],
-                    at.part_device(dx, dy),
-                )
-            move.start()
-            moves.append(move)
     vb(4)
     va(2)
     va(-2)
@@ -683,6 +735,25 @@
     vc(1)
     vc(-1)
     vz(4)
+    for number, (src, dst) in enumerate([(o_ref, ao_ref), (dq_ref, gq_ref)]):
+        for place, (dx, dy) in enumerate(at.offsets):
+            xh, y = at.part_of(dx, dy)
+            piece = src.at[xh * YN + y]
+            slot = dst.at[
+                pl.ds(pl.multiple_of(at.xh * HALF, HALF), HALF), lanes(at.y, GROUP * HD)
+            ]
+            if place == 0:
+                move = pltpu.make_async_copy(piece, slot, local.at[number])
+            else:
+                move = remote(
+                    piece,
+                    slot,
+                    p_send.at[number, place],
+                    p_recv.at[number, place],
+                    at.part_device(dx, dy),
+                )
+            move.start()
+            moves.append(move)
     k_step = kz_step(k_step, 4)
     vc(0)
 

time: 258 us -> 203 us (0.79)
  Pallas kernels: 248 us -> 193 us
    pallas_call x1, Pallas kernels: 78.1 us -> 32.7 us  [attention(): pl.pallas_call(attention_kernel, out_shape=(part_shape, part_shape, whole...]
    pallas_call x1, Pallas kernels: 84.5 us -> 74.5 us  [gather(): pl.pallas_call(gather_kernel, out_shape=(whole, whole, part, part), in_sp...]
where the time goes in v2:
time: 203 us
  Pallas kernels  193 us (95%)
  local copies, waits for them, and re-layouts  6.4 us (3%)
  other arithmetic  2.47 us (1%)
    pallas_call x1, Pallas kernels, scatter(): pl.pallas_call(scatter_kernel, out_shape=(tokens, tokens, pairs, pairs),...  86.1 us
    pallas_call x1, Pallas kernels, gather(): pl.pallas_call(gather_kernel, out_shape=(whole, whole, part, part), in_sp...  74.5 us
    pallas_call x1, Pallas kernels, attention(): pl.pallas_call(attention_kernel, out_shape=(part_shape, part_shape, whole...  32.7 us
    unnamed x10, local copies, waits for them, and re-layouts  4.98 us

profile of v2, /device:TPU:2, one launch (start us, length us, event | category | flops | bytes accessed | tf_op | source)
XLA Modules:
  0.0 203.0 jit_solution(646430521860574853)
XLA Ops:
  0.7 0.1 iota_add_fusion
  0.8 0.7 copy.11
  1.5 0.1 reduce-window.8
  1.6 0.1 reduce
  1.7 0.8 select_reduce_fusion
  2.4 0.7 tile.9.start_ref
  3.1 0.1 slice_reduce_fusion
  3.3 0.1 select_reduce_fusion.2
  3.4 0.0 copy-start.2
  3.4 0.5 compare_select_fusion.first_use
  3.9 0.7 pad_add_fusion.meta
  4.6 74.5 %gather.1 = (bf16[2,4,2,8,2,128,128]{6,5,4,3,2,1,0:T(8,128)(2,1)}, bf16[2,4,2,8,2,128,128]{6,5,4,3,2,1,0:T(8,128)(2,1)}, bf16[8,64,512]{2,1,0:T(8,128)(2,1)}, bf16[8,64,512]{2,1,0:T(8,128)(2,1)}) custom-call(bf16[128,2048]{1,0:T(8,128)(2,1)} %q_ref.1, bf16[128,512]{1,0:T(8,128)(2,1)} %k_ref.1, bf16[128,512]{1,0:T(8,128)(2,1)} %v_ref.1, bf16[128,2048]{1,0:T(8,128)(2,1)} %g_ref.1), custom_call_target="tpu_custom_call" | custom-call | tf_op jit(solution)/shard_map/gather/pallas_call | solution.py:271
  79.2 0.0 copy-done.2
  79.2 32.7 %attention.1 = (bf16[8,64,512]{2,1,0:T(8,128)(2,1)}, bf16[8,64,512]{2,1,0:T(8,128)(2,1)}, bf16[32768,128]{1,0:T(8,128)(2,1)}, bf16[32768,128]{1,0:T(8,128)(2,1)}) custom-call(s32[8,4]{1,0:T(8,128)} %pad_add_fusion.meta, s32[64]{0:T(128)} %compare_select_fusion.first_use, s32[64]{0:T(128)} %copy-done.2, s32[8,1,256]{2,1,0:T(1,128)} %tile.9.start_ref, ...), custom_call_target="tpu_custom_call" | custom-call | tf_op jit(solution)/shard_map/attention/pallas_call | solution.py:514
  111.9 0.0 copy-start
  111.9 1.0 copy-done
  112.9 0.0 copy-start.1
  112.9 1.0 copy-done.1
  114.0 86.1 %scatter.1 = (bf16[128,2048]{1,0:T(8,128)(2,1)S(1)}, bf16[128,2048]{1,0:T(8,128)(2,1)S(1)}, bf16[128,512]{1,0:T(8,128)(2,1)S(1)}, bf16[128,512]{1,0:T(8,128)(2,1)S(1)}) custom-call(bf16[8,64,512]{2,1,0:T(8,128)(2,1)S(1)} %copy-done, bf16[8,64,512]{2,1,0:T(8,128)(2,1)S(1)} %copy-done.1, bf16[2,4,2,8,2,128,128]{6,5,4,3,2,1,0:T(8,128)(2,1)} %bitcast.7, ...), custom_call_target="tpu_custom_call" | custom-call | tf_op jit(solution)/shard_map/scatter/pallas_call | solution.py:810
  200.1 0.8 copy.16
  200.9 0.8 copy.17
  201.7 0.7 copy.18
  202.3 0.7 copy.19
  (4 shorter events, 0.1 us)
Async XLA Ops:
  3.4 75.8 %copy-start.2 = (s32[64]{0:T(128)}, s32[64]{0:T(128)S(1)}, u32[]{:S(2)}) copy-start(s32[64]{0:T(128)S(1)} %get-tuple-element.20.last_use) | copy-start | bytes 772
  111.9 1.0 copy-start
  112.9 1.0 copy-start.1

commit v3 on v2

--- a/solution.py
+++ b/solution.py
@@ -25,7 +25,7 @@
 UNITS = 4
 KBLOCKS = SEQ // KB
 SPAN = (DOC_MOST + HALF - 1 + KB - 1) // KB
-FLUSH_SLOTS = 4
+FLUSH_SLOTS = 8
 
 MESH = pl.DeviceIdType.MESH
 ANY = pl.BlockSpec(memory_space=pl.ANY)
@@ -67,6 +67,7 @@
         self.x, self.y, self.z, self.core = here()
         self.xh, self.xl = self.x // 2, lax.rem(self.x, 2)
         self.x_peer = [device(self.x_at(d), self.y, self.z, self.core) for d in (1, -1)]
+        self.row_peer = self.x_peer + [device(self.x_at(2), self.y, self.z, self.core)]
         self.z_peer = [device(self.x, self.y, self.z_at(d), self.core) for d in (1, -1)]
         self.partner = device(self.x, self.y, self.z, 1 - self.core)
         self.offsets = [(dx, dy) for dx in range(XHI) for dy in range(YN)]
@@ -141,8 +142,8 @@
         number = len(crossing)
         crossing.append(go(piece, c_send.at[number], c_recv.at[number], at.partner))
 
-    def kx(number, piece, way):
-        return go(piece, kx_send.at[number], kx_recv.at[number], at.x_peer[way])
+    def kx(way, piece):
+        return go(piece, kx_send.at[way], kx_recv.at[way], at.row_peer[way])
 
     def kz(step, half, way):
         dz = (1 - step) if way == 0 else (step - 1)
@@ -191,14 +192,10 @@
 
     for copy in copies[0]:
         copy.wait()
-    k_first = [kx(way, at.chunk(ka_ref, 0, 0), way) for way in range(2)]
+    k_first = [kx(way, at.chunk(ka_ref, 0, 0)) for way in range(3)]
     for copy in copies[1]:
         copy.wait()
     v_step = [vz(1, way) for way in range(2)]
-    k_second = []
-    for way in range(2):
-        k_first[way].wait_recv()
-        k_second.append(kx(2 + way, at.chunk(ka_ref, 2 * way - 1, 0, way), way))
     vx_start(0)
 
     def vz_next(step):
@@ -208,20 +205,20 @@
             vx_start((1 - step) if way == 0 else (step - 1))
 
     vz_next(2)
-    for copy in k_second:
+    for copy in k_first:
         copy.wait_recv()
     k_step = {(half, way): kz(1, half, way) for half in range(2) for way in range(2)}
     cross(at.across_x(ka_ref, at.core, 0))
     vz_next(3)
     vx_forward(0)
     vz_next(4)
+    k_step = kz_step(k_step, 2)
     vx_forward(-1)
     vx_forward(1)
     vx_end(0)
     for way in range(2):
         v_step[way].wait_recv()
     vx_start(4)
-    k_step = kz_step(k_step, 2)
     vx_forward(-2)
     vx_forward(2)
     vx_end(-1)
@@ -547,7 +544,7 @@
 
 def scatter_kernel(
     o_ref, dq_ref, dk_ref, dv_ref, ao_ref, gq_ref, gk_ref, gv_ref,
-    own, part, kz_in, kx_half, kx_in, vx_half, vx_in, vz_in,
+    own, part, kz_in, kx_in, vx_half, vx_in, vz_in,
     own_sem, c_send, c_recv, kz_send, kz_recv, kx_send, kx_recv, vx_send, vx_recv,
     vz_send, vz_recv, p_send, p_recv, y_send, y_recv, local,
 ):
@@ -783,15 +780,28 @@
         where = (0, 3, slice(None), halves(half))
         total = f32(own[where]) + f32(kz_in[0, 3, half]) + f32(kz_in[1, 3, half])
         own[where] = total.astype(jnp.bfloat16)
-    first = x_first(0, 0, kx_half, kx_send, kx_recv)
+    row = [
+        go(
+            own.at[own_chunk(0, 0, dx)],
+            kx_in.at[way],
+            kx_send.at[way],
+            kx_recv.at[way],
+            at.row_peer[way],
+        )
+        for way, dx in enumerate((1, -1, 2))
+    ]
     for way in range(2):
         v_step[way].wait_recv()
     mine = own_chunk(1, 0, 0)
     total = f32(own[mine]) + f32(vz_in[0, 3]) + f32(vz_in[1, 3])
     own[mine] = total.astype(jnp.bfloat16)
     finish(1, gv_ref)
-    second = x_second(0, 0, first, kx_half, kx_in, kx_send, kx_recv)
-    x_third(0, 0, second, kx_in)
+    mine = own_chunk(0, 0, 0)
+    total = f32(own[mine])
+    for way in range(3):
+        row[way].wait_recv()
+        total = total + f32(kx_in[way])
+    own[mine] = total.astype(jnp.bfloat16)
     finish(0, gk_ref)
     for move in moves:
         move.wait()
@@ -816,13 +826,12 @@
             box(2, ZN, XHI, YN, XLO),
             box(2, ZN, XHI, YN, XLO),
             box(2, 4, 2, XHI, 2, XLO),
-            box(2, 2),
-            box(2, YN),
+            box(3, YN),
             box(ZN, 2, 2),
             box(ZN, 2, YN),
             box(2, 4, YN),
             dma((2, ZN)), dma((2, ZN)), dma((2, ZN)), dma((2, 4, 2)), dma((2, 4, 2)),
-            dma((2, 2)), dma((2, 2)), dma((2, ZN, 2)), dma((2, ZN, 2)), dma((2, 4)), dma((2, 4)),
+            dma((3,)), dma((3,)), dma((2, ZN, 2)), dma((2, ZN, 2)), dma((2, 4)), dma((2, 4)),
             dma((2, PIECES)), dma((2, PIECES)), dma((2, YN)), dma((2, YN)), dma((4,)),
         ],
         compiler_params=pltpu.CompilerParams(

time: 203 us -> 199 us (0.980); the launches traced: 203 us -> 196 us
  Pallas kernels: 193 us -> 187 us
    pallas_call x1, Pallas kernels: 86.1 us -> 75.5 us  [scatter(): pl.pallas_call(scatter_kernel, out_shape=(tokens, tokens, pairs, pairs),...]
    pallas_call x1, Pallas kernels: 32.7 us -> 39.8 us  [attention(): pl.pallas_call(attention_kernel, out_shape=(part_shape, part_shape, whole...]
    pallas_call x1, Pallas kernels: 74.5 us -> 71.4 us  [gather(): pl.pallas_call(gather_kernel, out_shape=(whole, whole, part, part), in_sp...]
where the time goes in v3:
time: 199 us; the launch traced here: 196 us
  Pallas kernels  187 us (94%)
  local copies, waits for them, and re-layouts  6.4 us (3%)
  other arithmetic  2.47 us (1%)
    pallas_call x1, Pallas kernels, scatter(): pl.pallas_call(scatter_kernel, out_shape=(tokens, tokens, pairs, pairs),...  75.5 us
    pallas_call x1, Pallas kernels, gather(): pl.pallas_call(gather_kernel, out_shape=(whole, whole, part, part), in_sp...  71.4 us
    pallas_call x1, Pallas kernels, attention(): pl.pallas_call(attention_kernel, out_shape=(part_shape, part_shape, whole...  39.8 us
    unnamed x10, local copies, waits for them, and re-layouts  4.98 us

profile of v3, /device:TPU:2, one launch (start us, length us, event | category | flops | bytes accessed | tf_op | source)
XLA Modules:
  0.0 196.4 jit_solution(4765957053185892266)
XLA Ops:
  0.7 0.1 iota_add_fusion
  0.8 0.7 copy.11
  1.5 0.1 reduce-window.8
  1.6 0.1 reduce
  1.7 0.8 select_reduce_fusion
  2.4 0.7 tile.9.start_ref
  3.1 0.1 slice_reduce_fusion
  3.3 0.1 select_reduce_fusion.2
  3.4 0.0 copy-start.2
  3.4 0.5 compare_select_fusion.first_use
  3.9 0.7 pad_add_fusion.meta
  4.6 71.4 %gather.1 = (bf16[2,4,2,8,2,128,128]{6,5,4,3,2,1,0:T(8,128)(2,1)}, bf16[2,4,2,8,2,128,128]{6,5,4,3,2,1,0:T(8,128)(2,1)}, bf16[8,64,512]{2,1,0:T(8,128)(2,1)}, bf16[8,64,512]{2,1,0:T(8,128)(2,1)}) custom-call(bf16[128,2048]{1,0:T(8,128)(2,1)} %q_ref.1, bf16[128,512]{1,0:T(8,128)(2,1)} %k_ref.1, bf16[128,512]{1,0:T(8,128)(2,1)} %v_ref.1, bf16[128,2048]{1,0:T(8,128)(2,1)} %g_ref.1), custom_call_target="tpu_custom_call" | custom-call | tf_op jit(solution)/shard_map/gather/pallas_call | solution.py:268
  76.1 0.0 copy-done.2
  76.1 39.8 %attention.1 = (bf16[8,64,512]{2,1,0:T(8,128)(2,1)}, bf16[8,64,512]{2,1,0:T(8,128)(2,1)}, bf16[32768,128]{1,0:T(8,128)(2,1)}, bf16[32768,128]{1,0:T(8,128)(2,1)}) custom-call(s32[8,4]{1,0:T(8,128)} %pad_add_fusion.meta, s32[64]{0:T(128)} %compare_select_fusion.first_use, s32[64]{0:T(128)} %copy-done.2, s32[8,1,256]{2,1,0:T(1,128)} %tile.9.start_ref, ...), custom_call_target="tpu_custom_call" | custom-call | tf_op jit(solution)/shard_map/attention/pallas_call | solution.py:511
  115.9 0.0 copy-start
  115.9 1.0 copy-done
  116.9 0.0 copy-start.1
  116.9 1.0 copy-done.1
  118.0 75.5 %scatter.1 = (bf16[128,2048]{1,0:T(8,128)(2,1)S(1)}, bf16[128,2048]{1,0:T(8,128)(2,1)S(1)}, bf16[128,512]{1,0:T(8,128)(2,1)S(1)}, bf16[128,512]{1,0:T(8,128)(2,1)S(1)}) custom-call(bf16[8,64,512]{2,1,0:T(8,128)(2,1)S(1)} %copy-done, bf16[8,64,512]{2,1,0:T(8,128)(2,1)S(1)} %copy-done.1, bf16[2,4,2,8,2,128,128]{6,5,4,3,2,1,0:T(8,128)(2,1)} %bitcast.7, ...), custom_call_target="tpu_custom_call" | custom-call | tf_op jit(solution)/shard_map/scatter/pallas_call | solution.py:820
  193.5 0.8 copy.16
  194.3 0.8 copy.17
  195.1 0.7 copy.18
  195.7 0.7 copy.19
  (4 shorter events, 0.1 us)
Async XLA Ops:
  3.4 72.7 %copy-start.2 = (s32[64]{0:T(128)}, s32[64]{0:T(128)S(1)}, u32[]{:S(2)}) copy-start(s32[64]{0:T(128)S(1)} %get-tuple-element.20.last_use) | copy-start | bytes 772
  115.9 1.0 copy-start
  116.9 1.0 copy-start.1

commit v4 on v3

--- a/solution.py
+++ b/solution.py
@@ -281,9 +281,9 @@
 
 
 def attention_kernel(
-    meta, first_use, last_use, start_ref, q_ref, g_ref, ka_ref, va_ref, o_ref, dq_ref, dk_ref,
-    dv_ref, kbuf, vbuf, sbuf, pbuf, dk_acc, dv_acc, flush, zeros, pending, k_sem, v_sem, f_sem,
-    z_sem,
+    meta, start_ref, q_ref, g_ref, ka_ref, va_ref, o_ref, dq_ref, dk_ref, dv_ref,
+    kbuf, vbuf, sbuf, pbuf, dk_acc, dv_acc, flush, zeros, result, pending, first_use, last_use,
+    k_sem, v_sem, f_sem, z_sem, o_sem,
 ):
     scaling = HD ** (-0.5)
     factor = scaling * math.log2(math.e)
@@ -348,7 +348,36 @@
             pltpu.make_async_copy(flush.at[1, slot], dv_ref.at[block(kb)], f_sem.at[1, slot]),
         )
 
+    def results(i, slot):
+        return (
+            pltpu.make_async_copy(result.at[0, slot], o_ref.at[i], o_sem.at[0, slot]),
+            pltpu.make_async_copy(result.at[1, slot], dq_ref.at[i], o_sem.at[1, slot]),
+        )
+
+    def blocks_of(i):
+        low, count = meta[i, 0], meta[i, 1]
+        return low // KB, (low + count * KB - 1) // KB + 1
+
     fetch(0, 0)
+
+    def unused(kb, carry):
+        first_use[kb] = -1
+        last_use[kb] = -1
+        return carry
+
+    lax.fori_loop(0, KBLOCKS, unused, 0)
+
+    def mark_piece(i, carry):
+        def mark(kb, carry):
+            last_use[kb] = i
+            seen = first_use[kb]
+            first_use[kb] = jnp.where(seen < 0, i, seen)
+            return carry
+
+        lax.fori_loop(*blocks_of(i), mark, 0)
+        return carry
+
+    lax.fori_loop(0, PIECES, mark_piece, 0)
     zeros[...] = jnp.zeros((KB, HD), jnp.bfloat16)
     for slot in range(FLUSH_SLOTS):
         pending[slot] = 0
@@ -416,11 +445,17 @@
         )
         inverse = 1.0 / jnp.sum(total, axis=0, keepdims=True)
         out = (out * inverse).astype(jnp.bfloat16).astype(jnp.float32)
-        o_ref[i] = unstacked(out.T.astype(jnp.bfloat16))
+
+        @pl.when(i >= 2)
+        def _():
+            for copy in results(i - 2, slot):
+                copy.wait()
+
+        result[0, slot] = unstacked(out.T.astype(jnp.bfloat16))
         g_turned = g.astype(jnp.float32).T
         delta = jnp.sum(g_turned * out, axis=0, keepdims=True) * inverse
         g_rows = (g_turned * inverse).T.astype(jnp.bfloat16)
-        block_low, block_end = low // KB, (low + count * KB - 1) // KB + 1
+        block_low, block_end = blocks_of(i)
 
         def clear(kb, carry):
             @pl.when(first_use[kb] == i)
@@ -443,7 +478,9 @@
             return dq + mm(k, ds, 0, 0)
 
         dq = in_pairs(count, grad_step, jnp.zeros((HD, ROWS), jnp.float32))
-        dq_ref[i] = unstacked((dq * scaling).T.astype(jnp.bfloat16))
+        result[1, slot] = unstacked((dq * scaling).T.astype(jnp.bfloat16))
+        for copy in results(i, slot):
+            copy.start()
 
         def flush_step(kb, carry):
             @pl.when(last_use[kb] == i)
@@ -467,6 +504,9 @@
         return carry
 
     lax.fori_loop(0, PIECES, piece, 0)
+    for i in (PIECES - 2, PIECES - 1):
+        for copy in results(i, i % 2):
+            copy.wait()
     for slot in range(FLUSH_SLOTS):
 
         @pl.when(pending[slot] > 0)
@@ -491,7 +531,7 @@
     part = jnp.arange(PIECES, dtype=jnp.int32)
     tile = (part // YN) * 128 + lax.rem(part, YN) * 32 + core * 16 + z * 2 + lax.rem(x, 2)
     first = tile * 128 + (x // 2) * HALF
-    times = first[:, None] + jnp.arange(HALF, dtype=jnp.int32)[None, :]
+    times = first[:, None] + lax.rem(jnp.arange(ROWS, dtype=jnp.int32), HALF)[None, :]
     starts = jnp.sum(
         jnp.where(ends[None, None, :] <= times[:, :, None], lengths[None, None, :], 0), axis=2
     )
@@ -499,20 +539,15 @@
     count = (end - starts[:, 0] + KB - 1) // KB
     low = jnp.maximum(end - count * KB, 0)
     meta = jnp.stack([low, count, first, starts[:, HALF - 1]], axis=1).astype(jnp.int32)
-    ids = jnp.arange(KBLOCKS, dtype=jnp.int32)[:, None]
-    used = (ids >= low[None] // KB) & (ids <= (low + count * KB - 1)[None] // KB)
-    last_use = jnp.max(jnp.where(used, part[None], -1), axis=1)
-    first_use = jnp.min(jnp.where(used, part[None], PIECES), axis=1)
-    first_use = jnp.where(last_use < 0, -1, first_use)
-    start_rows = jnp.tile(starts, (1, GROUP)).reshape(PIECES, 1, ROWS).astype(jnp.int32)
+    start_rows = starts.reshape(PIECES, 1, ROWS).astype(jnp.int32)
     part_shape = jax.ShapeDtypeStruct((PIECES, HALF, GROUP * HD), jnp.bfloat16)
     whole = jax.ShapeDtypeStruct((SEQ, HD), jnp.bfloat16)
     dma = pltpu.SemaphoreType.DMA
     return pl.pallas_call(
         attention_kernel,
         out_shape=(part_shape, part_shape, whole, whole),
-        in_specs=[SMEM, SMEM, SMEM, VMEM, VMEM, VMEM, ANY, ANY],
-        out_specs=(VMEM, VMEM, ANY, ANY),
+        in_specs=[SMEM, VMEM, VMEM, VMEM, ANY, ANY],
+        out_specs=(ANY,) * 4,
         scratch_shapes=[
             pltpu.VMEM((2, SPAN * KB, HD), jnp.bfloat16),
             pltpu.VMEM((2, SPAN * KB, HD), jnp.bfloat16),
@@ -522,18 +557,20 @@
             pltpu.VMEM((SEQ, HD), jnp.float32),
             pltpu.VMEM((2, FLUSH_SLOTS, KB, HD), jnp.bfloat16),
             pltpu.VMEM((KB, HD), jnp.bfloat16),
+            pltpu.VMEM((2, 2, HALF, GROUP * HD), jnp.bfloat16),
             pltpu.SMEM((FLUSH_SLOTS,), jnp.int32),
+            pltpu.SMEM((KBLOCKS,), jnp.int32),
+            pltpu.SMEM((KBLOCKS,), jnp.int32),
             dma((2, SPAN)),
             dma((2, SPAN)),
             dma((2, FLUSH_SLOTS)),
             dma((2, KBLOCKS)),
+            dma((2, 2)),
         ],
         compiler_params=pltpu.CompilerParams(vmem_limit_bytes=62 << 20),
         name="attention",
     )(
         meta,
-        first_use.astype(jnp.int32),
-        last_use.astype(jnp.int32),
         start_rows,
         q,
         g,

time: 199 us -> 198 us (level)
    unnamed x10 -> x8, local copies, waits for them, and re-layouts: 4.98 us -> 4.98 us
where the time goes in v4:
time: 198 us; the launch traced here: 196 us
  Pallas kernels  188 us (95%)
  local copies, waits for them, and re-layouts  6.32 us (3%)
    pallas_call x1, Pallas kernels, scatter(): pl.pallas_call(scatter_kernel, out_shape=(tokens, tokens, pairs, pairs),...  75.2 us
    pallas_call x1, Pallas kernels, gather(): pl.pallas_call(gather_kernel, out_shape=(whole, whole, part, part), in_sp...  71.4 us
    pallas_call x1, Pallas kernels, attention(): pl.pallas_call(attention_kernel, out_shape=(part_shape, part_shape, whole...  41 us
    unnamed x8, local copies, waits for them, and re-layouts  4.98 us

profile of v4, /device:TPU:2, one launch (start us, length us, event | category | flops | bytes accessed | tf_op | source)
XLA Modules:
  0.0 196.5 jit_solution(17783807260653338230)
XLA Ops:
  0.7 0.1 broadcast_add_fusion
  0.8 0.7 copy.11
  1.5 0.1 reduce-window.8
  1.6 0.1 reduce
  1.7 0.8 select_reduce_fusion
  2.5 0.6 reshape.145.start_ref
  3.1 0.1 subtract_maximum_fusion
  3.1 0.7 pad_add_fusion.meta
  3.8 71.4 %gather.1 = (bf16[2,4,2,8,2,128,128]{6,5,4,3,2,1,0:T(8,128)(2,1)}, bf16[2,4,2,8,2,128,128]{6,5,4,3,2,1,0:T(8,128)(2,1)}, bf16[8,64,512]{2,1,0:T(8,128)(2,1)}, bf16[8,64,512]{2,1,0:T(8,128)(2,1)}) custom-call(bf16[128,2048]{1,0:T(8,128)(2,1)} %q_ref.1, bf16[128,512]{1,0:T(8,128)(2,1)} %k_ref.1, bf16[128,512]{1,0:T(8,128)(2,1)} %v_ref.1, bf16[128,2048]{1,0:T(8,128)(2,1)} %g_ref.1), custom_call_target="tpu_custom_call" | custom-call | tf_op jit(solution)/shard_map/gather/pallas_call | solution.py:268
  75.3 41.0 %attention.1 = (bf16[8,64,512]{2,1,0:T(8,128)(2,1)}, bf16[8,64,512]{2,1,0:T(8,128)(2,1)}, bf16[32768,128]{1,0:T(8,128)(2,1)}, bf16[32768,128]{1,0:T(8,128)(2,1)}) custom-call(s32[8,4]{1,0:T(8,128)} %pad_add_fusion.meta, s32[8,1,256]{2,1,0:T(1,128)} %reshape.145.start_ref, bf16[8,64,512]{2,1,0:T(8,128)(2,1)} %get-tuple-element.12.q_ref, ...), custom_call_target="tpu_custom_call" | custom-call | tf_op jit(solution)/shard_map/attention/pallas_call | solution.py:546
  116.2 0.0 copy-start
  116.2 1.0 copy-done
  117.3 0.0 copy-start.1
  117.3 1.0 copy-done.1
  118.3 75.2 %scatter.1 = (bf16[128,2048]{1,0:T(8,128)(2,1)S(1)}, bf16[128,2048]{1,0:T(8,128)(2,1)S(1)}, bf16[128,512]{1,0:T(8,128)(2,1)S(1)}, bf16[128,512]{1,0:T(8,128)(2,1)S(1)}) custom-call(bf16[8,64,512]{2,1,0:T(8,128)(2,1)S(1)} %copy-done, bf16[8,64,512]{2,1,0:T(8,128)(2,1)S(1)} %copy-done.1, bf16[2,4,2,8,2,128,128]{6,5,4,3,2,1,0:T(8,128)(2,1)} %bitcast.5, ...), custom_call_target="tpu_custom_call" | custom-call | tf_op jit(solution)/shard_map/scatter/pallas_call | solution.py:857
  193.6 0.8 copy.16
  194.3 0.8 copy.17
  195.1 0.7 copy.18
  195.8 0.7 copy.19
  (2 shorter events, 0.0 us)
Async XLA Ops:
  116.2 1.0 copy-start
  117.3 1.0 copy-start.1

commit v5 on v4

--- a/solution.py
+++ b/solution.py
@@ -872,7 +872,7 @@
             dma((2, PIECES)), dma((2, PIECES)), dma((2, YN)), dma((2, YN)), dma((4,)),
         ],
         compiler_params=pltpu.CompilerParams(
-            collective_id=1, has_side_effects=True, vmem_limit_bytes=48 << 20
+            collective_id=1, has_side_effects=True, vmem_limit_bytes=63 << 20
         ),
         name="scatter",
     )(out, dq, dk.reshape(WHOLE), dv.reshape(WHOLE))

time: 198 us -> 197 us (level)
  Pallas kernels: 188 us -> 185 us
    pallas_call x1, Pallas kernels: 41 us -> 32.8 us  [attention(): pl.pallas_call(attention_kernel, out_shape=(part_shape, part_shape, whole...]
    pallas_call x1, Pallas kernels: 75.2 us -> 81.1 us  [scatter(): pl.pallas_call(scatter_kernel, out_shape=(tokens, tokens, pairs, pairs),...]
    unnamed x8 -> x4, local copies, waits for them, and re-layouts: 4.98 us -> 6.9 us
where the time goes in v5:
time: 197 us; the launch traced here: 196 us
  Pallas kernels  185 us (94%)
  local copies, waits for them, and re-layouts  8.24 us (4%)
    pallas_call x1, Pallas kernels, scatter(): pl.pallas_call(scatter_kernel, out_shape=(tokens, tokens, pairs, pairs),...  81.1 us
    pallas_call x1, Pallas kernels, gather(): pl.pallas_call(gather_kernel, out_shape=(whole, whole, part, part), in_sp...  71.4 us
    pallas_call x1, Pallas kernels, attention(): pl.pallas_call(attention_kernel, out_shape=(part_shape, part_shape, whole...  32.8 us
    unnamed x4, local copies, waits for them, and re-layouts  6.9 us

profile of v5, /device:TPU:2, one launch (start us, length us, event | category | flops | bytes accessed | tf_op | source)
XLA Modules:
  0.0 196.1 jit_solution(15084473050736196399)
XLA Ops:
  0.7 0.1 broadcast_add_fusion
  0.8 0.7 copy.11
  1.5 0.1 reduce-window.8
  1.6 0.1 reduce
  1.7 0.8 select_reduce_fusion
  2.5 0.6 reshape.145.start_ref
  3.1 0.1 subtract_maximum_fusion
  3.1 0.7 pad_add_fusion.meta
  3.8 71.4 %gather.1 = (bf16[2,4,2,8,2,128,128]{6,5,4,3,2,1,0:T(8,128)(2,1)}, bf16[2,4,2,8,2,128,128]{6,5,4,3,2,1,0:T(8,128)(2,1)}, bf16[8,64,512]{2,1,0:T(8,128)(2,1)}, bf16[8,64,512]{2,1,0:T(8,128)(2,1)}) custom-call(bf16[128,2048]{1,0:T(8,128)(2,1)} %q_ref.1, bf16[128,512]{1,0:T(8,128)(2,1)} %k_ref.1, bf16[128,512]{1,0:T(8,128)(2,1)} %v_ref.1, bf16[128,2048]{1,0:T(8,128)(2,1)} %g_ref.1), custom_call_target="tpu_custom_call" | custom-call | tf_op jit(solution)/shard_map/gather/pallas_call | solution.py:268
  75.3 32.8 %attention.1 = (bf16[8,64,512]{2,1,0:T(8,128)(2,1)}, bf16[8,64,512]{2,1,0:T(8,128)(2,1)}, bf16[32768,128]{1,0:T(8,128)(2,1)}, bf16[32768,128]{1,0:T(8,128)(2,1)}) custom-call(s32[8,4]{1,0:T(8,128)} %pad_add_fusion.meta, s32[8,1,256]{2,1,0:T(1,128)} %reshape.145.start_ref, bf16[8,64,512]{2,1,0:T(8,128)(2,1)} %get-tuple-element.12.q_ref, ...), custom_call_target="tpu_custom_call" | custom-call | tf_op jit(solution)/shard_map/attention/pallas_call | solution.py:546
  108.0 81.1 %scatter.1 = (bf16[128,2048]{1,0:T(8,128)(2,1)}, bf16[128,2048]{1,0:T(8,128)(2,1)}, bf16[128,512]{1,0:T(8,128)(2,1)}, bf16[128,512]{1,0:T(8,128)(2,1)}) custom-call(bf16[8,64,512]{2,1,0:T(8,128)(2,1)} %get-tuple-element.16.o_ref, bf16[8,64,512]{2,1,0:T(8,128)(2,1)} %get-tuple-element.17.dq_ref, bf16[2,4,2,8,2,128,128]{6,5,4,3,2,1,0:T(8,128)(2,1)} %bitcast.5, ...), custom_call_target="tpu_custom_call" | custom-call | tf_op jit(solution)/shard_map/scatter/pallas_call | solution.py:857
  189.2 1.9 copy.16
  191.1 1.9 copy.17
  192.9 1.6 copy.18
  194.5 1.6 copy.19
  (2 shorter events, 0.0 us)
